TPU v7x, 256 devices: a whole 4x4x8 slice. The times are simulated.
256 devices in a mesh: row: 8 (over x, core), col: 32 (over y, z).
Axes of the slice: x: 4, y: 4, z: 8, core: 2. Of those that a mesh axis runs over, the one named last changes fastest.
Arguments:
- trailing: float32 [4096, 16384], P('row', 'col'), may hold values from -6 to 6
- panel_factors: float32 [4096, 256], P('row', 'col'), as said below
- pivots: int32 [256], replicated, may hold values from 0 to 4095, as said below
Outputs:
- applied: float32 [4096, 16384], P('row', 'col')
Inputs may be any that keep to these rules, and one draw needn't show every extreme that they name: pivots[j] lies between j and 4095. `panel_factors`: the strictly lower part of the first 256 rows keeps unit_lower well conditioned.
All inputs are finite; a program needn't handle non-finite values.
Results may differ from a plain program's by a relative error of at most 0.000059.
Values sent between devices are 32-bit elements; how exact they have to be, the bound alone decides.
No kernel may reach another device: no remote copies, remote signals or barrier semaphores. Data moves between devices by JAX's collectives and lax.ppermute only.
A program may use at most 64 MiB of HBM per device.

v0:
```python
import jax
import jax.numpy as jnp
from jax import lax
from jax.sharding import Mesh
from jax.sharding import PartitionSpec as P

ROW = ("row_0", "row_1")


def from_root(value, axes, root):
    value = jnp.where(lax.axis_index(axes) == root, value, jnp.zeros_like(value))
    for axis in axes:
        value = lax.psum(value, axis)
    return value


def joined_along(tiles, dim):
    tiles = jnp.moveaxis(tiles, 0, dim)
    shape = tiles.shape
    return tiles.reshape(*shape[:dim], shape[dim] * shape[dim + 1], *shape[dim + 2 :])


def from_everyone(value, axis):
    copies = jnp.broadcast_to(value, (lax.axis_size(axis), *value.shape))
    return lax.all_to_all(copies, axis, split_axis=0, concat_axis=0, tiled=True)


def gathered_copies(value, axis, dim):
    return joined_along(from_everyone(value, axis), dim)


def over_pieces(value, axis):
    tiles = lax.all_gather(value, axis)
    return tiles.sum(axis=0)


def slot_sources(pivots, width):
    column = jnp.arange(width, dtype=jnp.int32)
    equal = pivots[:, None] == pivots[None, :]
    first_hit = jnp.argmax(equal, axis=1)
    canon = jnp.where(pivots < width, pivots, width + first_hit)
    slot_ids = jnp.arange(2 * width, dtype=jnp.int32)[None, :]
    perms = jnp.where(
        slot_ids == column[:, None],
        canon[:, None],
        jnp.where(slot_ids == canon[:, None], column[:, None], slot_ids),
    )
    while perms.shape[0] > 1:
        perms = jnp.take_along_axis(perms[0::2], perms[1::2], axis=1)
    slot_pos = jnp.concatenate([column, pivots], axis=0)
    source = jnp.take(slot_pos, perms[0], axis=0)
    target_canon = (first_hit == column) & (pivots >= width)
    return (source, target_canon)


def on_device(trailing, panel_factors, pivots):
    rows_here = trailing.shape[0]
    panel_width = pivots.shape[0]
    first_row = lax.axis_index(ROW) * rows_here
    source, target_canon = slot_sources(pivots, panel_width)
    top_source = source[:panel_width]
    square_shard = from_root(panel_factors[:panel_width], ROW, 0)
    stacked = gathered_copies(jnp.concatenate([panel_factors, square_shard], axis=0), "col", 1)
    full_panel = stacked[:rows_here]
    diag_square = stacked[rows_here:]
    unit_lower = jnp.tril(diag_square, -1) + jnp.eye(panel_width, dtype=jnp.float32)
    local_index = top_source - first_row
    owned_rows = (local_index >= 0) & (local_index < rows_here)
    picked = jnp.take(trailing, jnp.clip(local_index, 0, rows_here - 1), axis=0)
    contrib = jnp.where(owned_rows[:, None], picked, 0.0)
    top_part = jnp.where(lax.axis_index(ROW) == 0, trailing[:panel_width], 0.0)
    pivot_block, old_top = (over_pieces(contrib, ROW), over_pieces(top_part, ROW))
    upper_rows = jax.scipy.linalg.solve_triangular(
        unit_lower, pivot_block, lower=True, unit_diagonal=True
    )
    update = trailing - jnp.dot(
        full_panel, upper_rows, precision=lax.Precision.HIGHEST, preferred_element_type=jnp.float32
    )
    target_local = pivots - first_row
    target_here = target_canon & (target_local >= 0) & (target_local < rows_here)
    target_index = jnp.clip(target_local, 0, rows_here - 1)
    moved_in = jnp.take(old_top, jnp.clip(source[panel_width:], 0, panel_width - 1), axis=0)
    replaced = jnp.take(trailing, target_index, axis=0)
    delta = jnp.where(target_here[:, None], moved_in - replaced, 0.0)
    update = update.at[target_index].add(delta)
    top_rows = jnp.where(lax.axis_index(ROW) == 0, upper_rows, update[:panel_width])
    return lax.dynamic_update_slice_in_dim(update, top_rows, 0, 0)


def solution(mesh):
    torus = Mesh(mesh.devices.reshape(4, 2, mesh.shape["col"]), ("row_0", "row_1", "col"))
    in_specs = (P(ROW, "col"), P(ROW, "col"), P())
    out_specs = P(ROW, "col")
    return jax.shard_map(
        on_device, mesh=torus, in_specs=in_specs, out_specs=out_specs, check_vma=False
    )
```

profile of v0, /device:TPU:1, one launch (start us, length us, event | category | flops | bytes accessed | tf_op | source)
XLA Modules:
  0.0 1140.1 jit_solution(6069349209698019796)
XLA Ops:
  6.5 1.5 iota_reduce_fusion
  9.7 518.5 %gather_fusion.2 = s32[65536]{0:T(1024)S(1)} fusion(s32[128,512]{1,0:T(8,128)S(1)} %slice.98, s32[65536]{0:T(1024)S(1)} %bitcast.97), kind=kCustom, calls=%fused_computation.5 | custom fusion | bytes 1048576 | tf_op jit(solution)/shard_map/jit(take_along_axis)/gather | solution.py:49
  528.6 258.4 %gather_fusion.3 = s32[32768]{0:T(1024)S(1)} fusion(s32[64,512]{1,0:T(8,128)S(1)} %slice.100, s32[32768]{0:T(1024)S(1)} %bitcast.98), kind=kCustom, calls=%fused_computation.6 | custom fusion | bytes 524288 | tf_op jit(solution)/shard_map/jit(take_along_axis)/gather | solution.py:49
  787.2 129.5 %gather_fusion.4 = s32[16384]{0:T(1024)S(1)} fusion(s32[32,512]{1,0:T(8,128)S(1)} %slice.102, s32[16384]{0:T(1024)S(1)} %bitcast.100), kind=kCustom, calls=%fused_computation.7 | custom fusion | bytes 262144 | tf_op jit(solution)/shard_map/jit(take_along_axis)/gather | solution.py:49
  916.8 65.0 %gather_fusion.5 = s32[8192]{0:T(1024)S(1)} fusion(s32[16,512]{1,0:T(8,128)S(1)} %slice.104, s32[8192]{0:T(1024)S(1)} %bitcast.101), kind=kCustom, calls=%fused_computation.8 | custom fusion | bytes 131072 | tf_op jit(solution)/shard_map/jit(take_along_axis)/gather | solution.py:49
  981.9 25.5 %gather_fusion.6 = s32[4096]{0:T(1024)S(1)} fusion(s32[8,512]{1,0:T(8,128)S(1)} %slice.106, s32[4096]{0:T(1024)S(1)} %bitcast.102), kind=kCustom, calls=%fused_computation.9 | custom fusion | bytes 65536 | tf_op jit(solution)/shard_map/jit(take_along_axis)/gather | solution.py:49
  1007.5 17.7 %gather_fusion.7 = s32[2048]{0:T(1024)S(1)} fusion(s32[4,512]{1,0:T(4,128)S(1)} %slice.108, s32[2048]{0:T(1024)S(1)} %bitcast.103), kind=kCustom, calls=%fused_computation.10 | custom fusion | bytes 32768 | tf_op jit(solution)/shard_map/jit(take_along_axis)/gather | solution.py:49
  1025.4 9.1 gather_fusion.8
  1034.6 3.5 gather_fusion
  1038.1 3.5 gather_fusion.1
  1044.7 9.4 psum.14
  1054.1 4.9 psum.15
  1059.9 11.4 all-to-all-start
  1071.3 18.6 %all-to-all-done = f32[32,768,8]{1,2,0:T(8,128)S(1)} async-done(((f32[32,768,8]{1,2,0:T(8,128)}), f32[32,768,8]{1,2,0:T(8,128)S(1)}, u32[]{:S(2)}, u32[]{:S(2)}) %all-to-all-start) | async-done | bytes 786464 | tf_op jit(solution)/shard_map/all_to_all | solution.py:25
  1090.0 4.3 while.1
  1090.6 1.4 dynamic-slice.7
  1092.8 1.4 dynamic-slice.7
  1094.3 19.7 %custom-call.4 = f32[2,128,128]{1,2,0:T(8,128)S(1)} custom-call(f32[2,128,128]{2,1,0:T(8,128)S(1)} %get-tuple-element.15), custom_call_target="InvertDiagBlocksLowerTriangular" | custom-call | tf_op jit(solution)/shard_map/jit(_solve_triangular)/triangular_solve | solution.py:73
  1114.0 2.7 reduce_sum.18
  1116.8 2.3 all-gather.7.cloned.1.call-done
  1119.1 3.5 reduce_sum.19
  1123.9 1.0 convolution_subtract_fusion
  1124.9 5.5 scatter_custom_fusion
  1131.4 1.9 fusion
  (94 shorter events, 10.2 us)
Async XLA Ops:
  6.5 1107.5 %all-gather.5.cloned.1.call-start = ((), (), s32[]{:S(2)}) async-start(), calls=%async_computation.1 | async-start | bytes 4718592 | tf_op jit(solution)/shard_map/all_gather | solution.py:33
  8.0 0.7 copy-start.4
  1007.5 17.8 %copy-start.3 = (s32[256]{0:T(256)S(1)}, s32[256]{0:T(256)}, u32[]{:S(2)}) copy-start(s32[256]{0:T(256)} %param.7) | copy-start | bytes 3076
  1025.4 16.3 %copy-start.5 = (s32[256]{0:T(256)S(1)}, s32[256]{0:T(256)}, u32[]{:S(2)}) copy-start(s32[256]{0:T(256)} %copy-done.4) | copy-start | bytes 3076
  1025.4 16.3 %copy-start = (f32[512,512]{1,0:T(8,128)S(1)}, f32[512,512]{1,0:T(8,128)}, u32[]{:S(2)}) copy-start(f32[512,512]{1,0:T(8,128)} %param.5) | copy-start | bytes 3145732
  1041.6 3.1 copy-start.2
  1043.7 75.4 %all-gather.7.cloned.1.call-start = ((), (), s32[]{:S(2)}) async-start(), calls=%async_computation.2 | async-start | bytes 4718592 | tf_op jit(solution)/shard_map/all_gather | solution.py:33
  1059.9 30.0 %all-to-all-start = ((f32[32,768,8]{1,2,0:T(8,128)}), f32[32,768,8]{1,2,0:T(8,128)S(1)}, u32[]{:S(2)}, u32[]{:S(2)}) async-start(f32[32,768,8]{1,2,0:T(8,128)} %broadcast_in_dim.124), calls=%async_computation | async-start | bytes 1572864 | tf_op jit(solution)/shard_map/all_to_all | solution.py:25
  1130.4 1.0 copy-start.1
Sparse Core Ops, SparseCore 0:
  1043.8 38.7 all-gather.4
  1084.5 34.5 all-gather.6
where the time goes:
time: 1140 us
  local copies, waits for them, and re-layouts  1040 us (91%)
  other arithmetic  38 us (3%)
  waiting for transfers between devices  20.9 us (2%)
  blocking collectives  14.3 us (1%)
  between operations  14 us (1%)
  starting transfers between devices  11.4 us (1%)
    gather x15, local copies, waits for them, and re-layouts, slot_sources(): perms = jnp.take_along_axis(perms[0::2], perms[1::2], axis=1)  1030 us
  transfers between devices with their start and end apart: 3, of which 2 were waited for; matrix products, arithmetic and copies ran while one was open for 3% of the time, Pallas kernels for 0%

commit v1 on v0

v1 whole, which is shorter than its diff:
```python
import jax
import jax.numpy as jnp
from jax import lax
from jax.experimental import pallas as pl
from jax.experimental.pallas import tpu as pltpu
from jax.sharding import Mesh
from jax.sharding import PartitionSpec as P

ROW = ("x", "core")
COL = ("y", "z")
HIGHEST = lax.Precision.HIGHEST
VMEM = pl.BlockSpec(memory_space=pltpu.VMEM)
SMEM = pl.BlockSpec(memory_space=pltpu.SMEM)


def f32(*shape):
    return jax.ShapeDtypeStruct(shape, jnp.float32)


def chip_shift(value, step):
    return lax.ppermute(value, "x", [(i, (i + step) % 4) for i in range(4)])


def core_swap(value):
    return lax.ppermute(value, "core", [(0, 1), (1, 0)])


def plan_kernel(piv, where_am_i, t_ref, keep, send, meta, source, displaced, order):
    width = piv.shape[0]
    half = width // 2
    rows = t_ref.shape[0]
    chip, core = where_am_i[0], where_am_i[1]
    device = chip * 2 + core
    first = device * rows

    def init(j, carry):
        p = piv[j]
        order[p] = p
        order[j] = j
        return carry

    lax.fori_loop(0, width, init, 0, unroll=8)

    def swap(j, carry):
        p = piv[j]
        a = order[j]
        b = order[p]
        order[j] = b
        order[p] = a
        return carry

    lax.fori_loop(0, width, swap, 0, unroll=8)

    def gather(i, out, slot):
        src = order[slot]
        down = order[src]
        source[slot] = src
        displaced[slot] = down
        meta[pl.ds(slot, 1), :] = jnp.full((1, 128), src, jnp.int32)
        own = (src >= first) & (src < first + rows)
        row = jnp.where(own, src - first, jnp.where(device == 0, down, 0))
        out[pl.ds(i, 1), :] = t_ref[pl.ds(row, 1), :]

    def both(i, carry):
        gather(i, send, (1 - core) * half + i)
        gather(i, keep, core * half + i)
        return carry

    lax.fori_loop(0, half, both, 0, unroll=4)


def owner_of(meta_rows, rows):
    device = meta_rows // rows
    device = jnp.concatenate([device] * 4, axis=1)
    return device // 2, device % 2


def combine_kernel(where_am_i, keep, got, meta, joined, p1, p2, p3):
    chip, core = where_am_i[0], where_am_i[1]
    half = keep.shape[0]
    part = half // 4
    owner_chip, owner_core = owner_of(meta[pl.ds(core * half, half), :], keep.shape[1])
    mine = owner_chip == chip
    other = (mine & (owner_core != core)) | (~mine & ((chip == 0) & (core == 1)))
    joined[...] = jnp.where(other, got[...], keep[...])
    for step, out in ((1, p1), (2, p2), (3, p3)):
        out[...] = joined[pl.ds(lax.rem(chip + step, 4) * part, part), :]


def route_kernel(where_am_i, joined, r1, r2, r3, meta, m0, m1, m2, m3):
    chip, core = where_am_i[0], where_am_i[1]
    half = joined.shape[0]
    part = half // 4
    owner_chip, _ = owner_of(
        meta[pl.ds(core * half + chip * part, part), :], joined.shape[1]
    )
    own = joined[pl.ds(chip * part, part), :]
    a, b, c = r1[...], r2[...], r3[...]
    behind = lax.rem(chip - owner_chip + 4, 4)
    pivot_row = jnp.where(
        behind == 0, own, jnp.where(behind == 1, a, jnp.where(behind == 2, b, c))
    )
    top_row = jnp.where(
        chip == 0, own, jnp.where(chip == 1, a, jnp.where(chip == 2, b, c))
    )
    for step, out in enumerate((m0, m1, m2, m3)):
        out[...] = jnp.where(
            owner_chip == lax.rem(chip + step, 4), top_row, pivot_row
        )


def halves_kernel(
    where_am_i, n0, n1, n2, n3, joined, keep, got, meta, message, pivot_half, top_half, g
):
    chip, core = where_am_i[0], where_am_i[1]
    half = joined.shape[0]
    part = half // 4
    for step, src in enumerate((n0, n1, n2, n3)):
        g[pl.ds(lax.rem(chip - step + 4, 4) * part, part), :] = src[...]
    owner_chip, owner_core = owner_of(meta[pl.ds(core * half, half), :], joined.shape[1])
    mine = owner_chip == chip
    routed = g[...]
    rows = joined[...]
    pivot_half[...] = jnp.where(mine, rows, routed)
    first_device = (chip == 0) & (core == 0)
    message[...] = jnp.where(
        mine & first_device,
        keep[...],
        jnp.where(mine & (owner_core == core), rows, routed),
    )
    top_half[...] = jnp.where(chip == 0, got[...], routed)


def final_kernel(
    where_am_i, source, displaced, t_ref, w_ref, pivot_half, top_half, send, got, meta, out, pivot
):
    chip, core = where_am_i[0], where_am_i[1]
    rows = t_ref.shape[0]
    half = pivot_half.shape[0]
    width = 2 * half
    device = chip * 2 + core
    first = device * rows
    out[...] = t_ref[...]

    def place(i, slot, tops):
        src = source[slot]

        @pl.when((src >= first) & (src < first + rows) & (src >= width))
        def _():
            @pl.when(device == 0)
            def _():
                out[pl.ds(src - first, 1), :] = t_ref[pl.ds(displaced[slot], 1), :]

            @pl.when(device != 0)
            def _():
                out[pl.ds(src - first, 1), :] = tops[pl.ds(i, 1), :]

    def both(i, carry):
        place(i, core * half + i, top_half)
        place(i, (1 - core) * half + i, got)
        return carry

    lax.fori_loop(0, half, both, 0, unroll=2)

    @pl.when(device == 0)
    def _():
        out[0:width, :] = jnp.zeros((width, out.shape[1]), jnp.float32)

    owner_chip, owner_core = owner_of(meta[pl.ds((1 - core) * half, half), :], rows)
    here = (owner_chip == chip) & (owner_core == core)
    pivot[pl.ds(core * half, half), :] = pivot_half[...]
    pivot[pl.ds((1 - core) * half, half), :] = jnp.where(here, send[...], got[...])
    out[...] -= jnp.dot(
        w_ref[...], pivot[...], precision=HIGHEST, preferred_element_type=jnp.float32
    )


def weights_kernel(where_am_i, stacked, w_ref):
    width = stacked.shape[0]
    rows = stacked.shape[1] - width
    square = stacked[:, rows:]
    row = lax.broadcasted_iota(jnp.int32, (width, width), 0)
    col = lax.broadcasted_iota(jnp.int32, (width, width), 1)
    inv = jnp.where(row == col, 1.0, 0.0)
    size = 1
    while size < width:
        link = (
            (row // (2 * size) == col // (2 * size))
            & (row // size % 2 == 0)
            & (col // size % 2 == 1)
        )
        off = jnp.where(link, square, 0.0)
        if size == 1:
            inv = inv - off
        else:
            left = jnp.dot(inv, off, precision=HIGHEST, preferred_element_type=jnp.float32)
            inv = inv - jnp.dot(
                left, inv, precision=HIGHEST, preferred_element_type=jnp.float32
            )
        size *= 2
    weights = jnp.dot(
        inv, stacked[:, :rows], precision=HIGHEST, preferred_element_type=jnp.float32
    )
    w_ref[...] = weights.T

    @pl.when((where_am_i[0] == 0) & (where_am_i[1] == 0))
    def _():
        w_ref[0:width, :] = -inv.T


def on_device(trailing, panel_factors, pivots):
    rows, columns = trailing.shape
    width = pivots.shape[0]
    half, part = width // 2, width // 8
    chip, core = lax.axis_index("x"), lax.axis_index("core")
    here = jnp.stack([chip, core]).astype(jnp.int32)

    panel = panel_factors.T
    square = panel[:, :width]
    square = jnp.where(core == 1, lax.ppermute(square, "core", [(0, 1)]), square)
    square = jnp.where(chip == 2, lax.ppermute(square, "x", [(0, 2)]), square)
    square = jnp.where(
        chip % 2 == 1, lax.ppermute(square, "x", [(0, 1), (2, 3)]), square
    )
    block = jnp.concatenate([panel, square], axis=1)
    copies = jnp.broadcast_to(block, (lax.axis_size(COL), *block.shape))
    stacked = lax.all_to_all(copies, COL, split_axis=0, concat_axis=0, tiled=True)
    stacked = stacked.reshape(width, rows + width)
    weights = pl.pallas_call(
        weights_kernel,
        out_shape=f32(rows, width),
        in_specs=[SMEM, VMEM],
        out_specs=VMEM,
    )(here, stacked)

    index = jax.ShapeDtypeStruct((width,), jnp.int32)
    keep, send, meta, source, displaced = pl.pallas_call(
        plan_kernel,
        out_shape=(
            f32(half, columns),
            f32(half, columns),
            jax.ShapeDtypeStruct((width, 128), jnp.int32),
            index,
            index,
        ),
        in_specs=[SMEM, SMEM, VMEM],
        out_specs=(VMEM, VMEM, VMEM, SMEM, SMEM),
        scratch_shapes=[pltpu.SMEM((rows * 8,), jnp.int32)],
    )(pivots, here, trailing)
    got = core_swap(send)
    joined, p1, p2, p3 = pl.pallas_call(
        combine_kernel,
        out_shape=(f32(half, columns),) + (f32(part, columns),) * 3,
        in_specs=[SMEM, VMEM, VMEM, VMEM],
        out_specs=(VMEM,) * 4,
    )(here, keep, got, meta)
    r1, r2, r3 = (chip_shift(p, s) for s, p in ((1, p1), (2, p2), (3, p3)))
    m0, m1, m2, m3 = pl.pallas_call(
        route_kernel,
        out_shape=(f32(part, columns),) * 4,
        in_specs=[SMEM] + [VMEM] * 5,
        out_specs=(VMEM,) * 4,
    )(here, joined, r1, r2, r3, meta)
    n1, n2, n3 = (chip_shift(m, s) for s, m in ((1, m1), (2, m2), (3, m3)))
    message, pivot_half, top_half = pl.pallas_call(
        halves_kernel,
        out_shape=(f32(half, columns),) * 3,
        in_specs=[SMEM] + [VMEM] * 8,
        out_specs=(VMEM,) * 3,
        scratch_shapes=[pltpu.VMEM((half, columns), jnp.float32)],
    )(here, m0, n1, n2, n3, joined, keep, got, meta)
    last = core_swap(message)
    return pl.pallas_call(
        final_kernel,
        out_shape=f32(rows, columns),
        in_specs=[SMEM, SMEM, SMEM] + [VMEM] * 7,
        out_specs=VMEM,
        scratch_shapes=[pltpu.VMEM((width, columns), jnp.float32)],
    )(here, source, displaced, trailing, weights, pivot_half, top_half, send, last, meta)


def solution(mesh):
    torus = Mesh(mesh.devices.reshape(4, 2, 4, 8), ("x", "core", "y", "z"))
    return jax.shard_map(
        on_device,
        mesh=torus,
        in_specs=(P(ROW, COL), P(ROW, COL), P()),
        out_specs=P(ROW, COL),
        check_vma=False,
    )
```

time: 1140 us -> 79.3 us (0.07)
  local copies, waits for them, and re-layouts: 1040 us -> 5.23 us
  other arithmetic: 38 us -> 0.68 us
  Pallas kernels: 0 us -> 28.6 us
  starting transfers between devices: 11.4 us -> 30.9 us
  blocking collectives: 14.3 us -> 0 us
  between operations: 14 us -> 0.09 us
    gather x17 -> x0, local copies, waits for them, and re-layouts: 1030 us -> none  [the longest x15 1030 us: slot_sources(): perms = jnp.take_along_axis(perms[0::2], perms[1::2], axis=1)]
    pallas_call x0 -> x6, Pallas kernels: none -> 28.6 us  [the longest x1 9.29 us: on_device(): pl.pallas_call(weights_kernel, out_shape=f32(rows, width), in_specs=[SMEM...]
    another operation x5 -> x1, other arithmetic: 21.2 us -> 0.67 us  [on_device(): here = jnp.stack([chip, core]).astype(jnp.int32)]
    ppermute x0 -> x11, starting transfers between devices: none -> 19.7 us  [the longest x6 9.17 us: chip_shift(): return lax.ppermute(value, 'x', [(i, (i + step) % 4) for i in range(4)])]
    all_to_all x1, waiting for transfers between devices: 18.6 us -> 0.01 us  [on_device(): lax.all_to_all(copies, COL, split_axis=0, concat_axis=0, tiled=True)]
    psum x2 -> x0, blocking collectives: 14.3 us -> none  [from_root(): value = lax.psum(value, axis)]
    ppermute x0 -> x11, waiting for transfers between devices: none -> 13.4 us  [the longest x6 6.65 us: chip_shift(): return lax.ppermute(value, 'x', [(i, (i + step) % 4) for i in range(4)])]
  transfers between devices with their start and end apart: 3 -> 12, of which waited for: 2 -> 10; matrix products, arithmetic and copies ran while one was open for 3% -> 1% of each run, Pallas kernels for 0% -> 27%
where the time goes in v1:
time: 79.3 us; the launch traced here: 78.8 us
  starting transfers between devices  30.9 us (39%)
  Pallas kernels  28.6 us (36%)
  waiting for transfers between devices  13.4 us (17%)
  local copies, waits for them, and re-layouts  5.23 us (7%)
    all_to_all x1, starting transfers between devices, on_device(): lax.all_to_all(copies, COL, split_axis=0, concat_axis=0, tiled=True)  11.2 us
    pallas_call x1, Pallas kernels, on_device(): pl.pallas_call(weights_kernel, out_shape=f32(rows, width), in_specs=[SMEM...  9.29 us
    ppermute x6, starting transfers between devices, chip_shift(): return lax.ppermute(value, 'x', [(i, (i + step) % 4) for i in range(4)])  9.17 us
    pallas_call x1, Pallas kernels, on_device(): pl.pallas_call(final_kernel, out_shape=f32(rows, columns), in_specs=[SMEM...  7.44 us
    ppermute x6, waiting for transfers between devices, chip_shift(): return lax.ppermute(value, 'x', [(i, (i + step) % 4) for i in range(4)])  6.65 us
    pallas_call x1, Pallas kernels, on_device(): pl.pallas_call(plan_kernel, out_shape=(f32(half, columns), f32(half, colu...  5.65 us
    ppermute x2, starting transfers between devices, core_swap(): return lax.ppermute(value, 'core', [(0, 1), (1, 0)])  4.55 us
    ppermute x1, waiting for transfers between devices, on_device(): lax.ppermute(square, 'core', [(0, 1)])  3.84 us
  transfers between devices with their start and end apart: 12, of which 10 were waited for; matrix products, arithmetic and copies ran while one was open for 1% of the time, Pallas kernels for 27%

profile of v1, /device:TPU:1, one launch (start us, length us, event | category | flops | bytes accessed | tf_op | source)
XLA Modules:
  0.0 78.8 jit_solution(10095476850041421253)
XLA Ops:
  0.8 1.3 %collective-permute-start = (f32[8,256]{1,0:T(8,128)S(1)}, f32[8,256]{1,0:T(8,128)S(1)}, u32[]{:S(2)}, u32[]{:S(2)}) collective-permute-start(f32[8,256]{1,0:T(8,128)S(1)} %slice.4), channel_id=1, source_target_pairs={{0,32},{1,33},{2,34},{3,35},{4,36},{5,37},{6,38},{7,39},{8,40},{9,... | collective-permute-start | bytes 24584 | tf_op jit(solution)/shard_map/ppermute | solution.py:220
  2.1 3.8 %collective-permute-done = f32[8,256]{1,0:T(8,128)S(1)} collective-permute-done((f32[8,256]{1,0:T(8,128)S(1)}, f32[8,256]{1,0:T(8,128)S(1)}, u32[]{:S(2)}, u32[]{:S(2)}) %collective-permute-start) | collective-permute-done | bytes 8224 | tf_op jit(solution)/shard_map/ppermute | solution.py:220
  5.9 3.4 %collective-permute-start.1 = (f32[8,256]{1,0:T(8,128)S(1)}, f32[8,256]{1,0:T(8,128)S(1)}, u32[]{:S(2)}, u32[]{:S(2)}) collective-permute-start(f32[8,256]{1,0:T(8,128)S(1)} %broadcast_select_fusion), channel_id=1, source_target_pairs={{0,128},{1,129},{2,130},{3,131},{4,132},{5,133},{6,134},{7,135},{8... | collective-permute-start | bytes 24584 | tf_op jit(solution)/shard_map/ppermute | solution.py:221
  10.1 1.3 %collective-permute-start.2 = (f32[8,256]{1,0:T(8,128)S(1)}, f32[8,256]{1,0:T(8,128)S(1)}, u32[]{:S(2)}, u32[]{:S(2)}) collective-permute-start(f32[8,256]{1,0:T(8,128)S(1)} %broadcast_select_fusion.1), channel_id=1, source_target_pairs={{0,64},{128,192},{1,65},{129,193},{2,66},{130,194},{3,67},{131,195... | collective-permute-start | bytes 24584 | tf_op jit(solution)/shard_map/ppermute | solution.py:223
  12.1 0.9 %broadcast_in_dim.3 = f32[32,8,768]{2,1,0:T(8,128)} broadcast(f32[8,768]{1,0:T(8,128)S(1)} %pad_maximum_fusion), dimensions={1,2} | broadcast | bytes 811008 | tf_op jit(solution)/shard_map/broadcast_in_dim | solution.py:226
  13.1 11.2 %all-to-all-start = ((f32[32,8,768]{2,1,0:T(8,128)}), f32[32,8,768]{2,1,0:T(8,128)S(1)}, u32[]{:S(2)}, u32[]{:S(2)}) async-start(f32[32,8,768]{2,1,0:T(8,128)} %broadcast_in_dim.3), calls=%async_computation | async-start | bytes 1572864 | tf_op jit(solution)/shard_map/all_to_all | solution.py:227
  25.0 5.7 %shard_map.37 = (f32[128,512]{1,0:T(8,128)}, f32[128,512]{1,0:T(8,128)}, s32[256,128]{1,0:T(8,128)}, s32[256]{0:T(256)}, s32[256]{0:T(256)}) custom-call(s32[256]{0:T(256)} %piv.1, s32[2]{0:T(128)} %pad_add_fusion.where_am_i, f32[512,512]{1,0:T(8,128)} %t_ref.3), custom_call_target="tpu_custom_call" | custom-call | tf_op jit(solution)/shard_map/pallas_call | solution.py:237
  30.6 2.0 %collective-permute-start.3 = (f32[128,512]{1,0:T(8,128)}, f32[128,512]{1,0:T(8,128)S(1)}, u32[]{:S(2)}, u32[]{:S(2)}) collective-permute-start(f32[128,512]{1,0:T(8,128)} %get-tuple-element.24.send), channel_id=1, source_target_pairs={{0,32},{32,0},{1,33},{33,1},{2,34},{34,2},{3,35},{35,3},{4,36},{36... | collective-permute-start | bytes 786440 | tf_op jit(solution)/shard_map/ppermute | solution.py:25
  32.6 1.4 %collective-permute-done.3.got = f32[128,512]{1,0:T(8,128)S(1)} collective-permute-done((f32[128,512]{1,0:T(8,128)}, f32[128,512]{1,0:T(8,128)S(1)}, u32[]{:S(2)}, u32[]{:S(2)}) %collective-permute-start.3) | collective-permute-done | bytes 262176 | tf_op jit(solution)/shard_map/ppermute | solution.py:25
  34.6 2.0 %shard_map.39 = (f32[128,512]{1,0:T(8,128)}, f32[32,512]{1,0:T(8,128)}, f32[32,512]{1,0:T(8,128)}, f32[32,512]{1,0:T(8,128)}) custom-call(s32[2]{0:T(128)} %pad_add_fusion.where_am_i, f32[128,512]{1,0:T(8,128)} %get-tuple-element.23.keep, f32[128,512]{1,0:T(8,128)} %copy-done.1, s32[256,128]{1,0:T(8,128)} %get-tuple-element.25.meta), custom_call_target="tpu_custom_call" | custom-call | tf_op jit(solution)/shard_map/pallas_call | solution.py:251
  36.7 2.0 %collective-permute-start.4 = (f32[32,512]{1,0:T(8,128)}, f32[32,512]{1,0:T(8,128)S(1)}, u32[]{:S(2)}, u32[]{:S(2)}) collective-permute-start(f32[32,512]{1,0:T(8,128)} %get-tuple-element.27), channel_id=1, source_target_pairs={{0,64},{64,128},{128,192},{192,0},{1,65},{65,129},{129,193},{193,1... | collective-permute-start | bytes 196616 | tf_op jit(solution)/shard_map/ppermute | solution.py:21
  38.7 3.5 %collective-permute-start.5 = (f32[32,512]{1,0:T(8,128)}, f32[32,512]{1,0:T(8,128)S(1)}, u32[]{:S(2)}, u32[]{:S(2)}) collective-permute-start(f32[32,512]{1,0:T(8,128)} %get-tuple-element.28), channel_id=1, source_target_pairs={{0,128},{64,192},{128,0},{192,64},{1,129},{65,193},{129,1},{193,65... | collective-permute-start | bytes 196616 | tf_op jit(solution)/shard_map/ppermute | solution.py:21
  42.2 1.1 %collective-permute-done.4.r1 = f32[32,512]{1,0:T(8,128)S(1)} collective-permute-done((f32[32,512]{1,0:T(8,128)}, f32[32,512]{1,0:T(8,128)S(1)}, u32[]{:S(2)}, u32[]{:S(2)}) %collective-permute-start.4) | collective-permute-done | bytes 65568 | tf_op jit(solution)/shard_map/ppermute | solution.py:21
  43.3 2.3 %collective-permute-done.5.r2 = f32[32,512]{1,0:T(8,128)S(1)} collective-permute-done((f32[32,512]{1,0:T(8,128)}, f32[32,512]{1,0:T(8,128)S(1)}, u32[]{:S(2)}, u32[]{:S(2)}) %collective-permute-start.5) | collective-permute-done | bytes 65568 | tf_op jit(solution)/shard_map/ppermute | solution.py:21
  46.4 1.9 %shard_map.40 = (f32[32,512]{1,0:T(8,128)}, f32[32,512]{1,0:T(8,128)}, f32[32,512]{1,0:T(8,128)}, f32[32,512]{1,0:T(8,128)}) custom-call(s32[2]{0:T(128)} %pad_add_fusion.where_am_i, f32[128,512]{1,0:T(8,128)} %get-tuple-element.26.joined, f32[32,512]{1,0:T(8,128)} %copy-done.7, f32[32,512]{1,0:T(8,128)} %copy-done.8, f32[32,512]{1,0:T(8,128)} %copy-done.9, ...), custom_call_target="tpu_custom_call" | custom-call | tf_op jit(solution)/shard_map/pallas_call | solution.py:258
  49.0 2.3 %collective-permute-start.8 = (f32[32,512]{1,0:T(8,128)}, f32[32,512]{1,0:T(8,128)S(1)}, u32[]{:S(2)}, u32[]{:S(2)}) collective-permute-start(f32[32,512]{1,0:T(8,128)} %get-tuple-element.32), channel_id=1, source_target_pairs={{0,128},{64,192},{128,0},{192,64},{1,129},{65,193},{129,1},{193,65... | collective-permute-start | bytes 196616 | tf_op jit(solution)/shard_map/ppermute | solution.py:21
  51.9 0.9 %collective-permute-done.7.n1 = f32[32,512]{1,0:T(8,128)S(1)} collective-permute-done((f32[32,512]{1,0:T(8,128)}, f32[32,512]{1,0:T(8,128)S(1)}, u32[]{:S(2)}, u32[]{:S(2)}) %collective-permute-start.7) | collective-permute-done | bytes 65568 | tf_op jit(solution)/shard_map/ppermute | solution.py:21
  52.8 1.1 %collective-permute-done.8.n2 = f32[32,512]{1,0:T(8,128)S(1)} collective-permute-done((f32[32,512]{1,0:T(8,128)}, f32[32,512]{1,0:T(8,128)S(1)}, u32[]{:S(2)}, u32[]{:S(2)}) %collective-permute-start.8) | collective-permute-done | bytes 65568 | tf_op jit(solution)/shard_map/ppermute | solution.py:21
  53.9 1.1 %collective-permute-done.9.n3 = f32[32,512]{1,0:T(8,128)S(1)} collective-permute-done((f32[32,512]{1,0:T(8,128)}, f32[32,512]{1,0:T(8,128)S(1)}, u32[]{:S(2)}, u32[]{:S(2)}) %collective-permute-start.9) | collective-permute-done | bytes 65568 | tf_op jit(solution)/shard_map/ppermute | solution.py:21
  55.6 2.3 %shard_map.41 = (f32[128,512]{1,0:T(8,128)}, f32[128,512]{1,0:T(8,128)}, f32[128,512]{1,0:T(8,128)}) custom-call(s32[2]{0:T(128)} %pad_add_fusion.where_am_i, f32[32,512]{1,0:T(8,128)} %get-tuple-element.30.n0, f32[32,512]{1,0:T(8,128)} %copy-done.3, f32[32,512]{1,0:T(8,128)} %copy-done.4, f32[32,512]{1,0:T(8,128)} %copy-done.5, ...), custom_call_target="tpu_custom_call" | custom-call | tf_op jit(solution)/shard_map/pallas_call | solution.py:265
  57.9 2.6 %collective-permute-start.10 = (f32[128,512]{1,0:T(8,128)}, f32[128,512]{1,0:T(8,128)S(1)}, u32[]{:S(2)}, u32[]{:S(2)}) collective-permute-start(f32[128,512]{1,0:T(8,128)} %get-tuple-element.36), channel_id=1, source_target_pairs={{0,32},{32,0},{1,33},{33,1},{2,34},{34,2},{3,35},{35,3},{4,36},{36... | collective-permute-start | bytes 786440 | tf_op jit(solution)/shard_map/ppermute | solution.py:25
  60.5 0.9 %copy-done = f32[32,8,768]{2,1,0:T(8,128)} copy-done((f32[32,8,768]{2,1,0:T(8,128)}, f32[32,8,768]{2,1,0:T(8,128)S(1)}, u32[]{:S(2)}) %copy-start) | copy-done | bytes 786456
  61.4 9.3 %shard_map.38.w_ref = f32[512,256]{1,0:T(8,128)} custom-call(s32[2]{0:T(128)} %pad_add_fusion.where_am_i, f32[256,768]{1,0:T(8,128)} %bitcast.4), custom_call_target="tpu_custom_call" | custom-call | tf_op jit(solution)/shard_map/pallas_call | solution.py:229
  71.4 7.4 %shard_map.42 = f32[512,512]{1,0:T(8,128)} custom-call(s32[2]{0:T(128)} %pad_add_fusion.where_am_i, s32[256]{0:T(256)} %get-tuple-element.21.source, s32[256]{0:T(256)} %get-tuple-element.22.displaced, f32[512,512]{1,0:T(8,128)} %t_ref.3, f32[512,256]{1,0:T(8,128)} %shard_map.38.w_ref, f32[128,512]{1,0:T(8,128)} %get-tuple-element.34.pivot_half, ...), custom_call_target="tpu_custom_call" | custom-call | tf_op jit(solution)/shard_map/pallas_call | solution.py:273
  (33 shorter events, 7.2 us)
Async XLA Ops:
  0.0 5.9 %copy-start.6 = (f32[512,8]{0,1:T(8,128)S(1)}, f32[512,8]{0,1:T(8,128)}, u32[]{:S(2)}) copy-start(f32[512,8]{0,1:T(8,128)} %param.4) | copy-start | bytes 49156
  0.8 5.1 %collective-permute-start = (f32[8,256]{1,0:T(8,128)S(1)}, f32[8,256]{1,0:T(8,128)S(1)}, u32[]{:S(2)}, u32[]{:S(2)}) collective-permute-start(f32[8,256]{1,0:T(8,128)S(1)} %slice.4), channel_id=1, source_target_pairs={{0,32},{1,33},{2,34},{3,35},{4,36},{5,37},{6,38},{7,39},{8,40},{9,... | collective-permute-start | bytes 24584 | tf_op jit(solution)/shard_map/ppermute | solution.py:220
  5.9 4.2 %collective-permute-start.1 = (f32[8,256]{1,0:T(8,128)S(1)}, f32[8,256]{1,0:T(8,128)S(1)}, u32[]{:S(2)}, u32[]{:S(2)}) collective-permute-start(f32[8,256]{1,0:T(8,128)S(1)} %broadcast_select_fusion), channel_id=1, source_target_pairs={{0,128},{1,129},{2,130},{3,131},{4,132},{5,133},{6,134},{7,135},{8... | collective-permute-start | bytes 24584 | tf_op jit(solution)/shard_map/ppermute | solution.py:221
  10.1 2.1 %collective-permute-start.2 = (f32[8,256]{1,0:T(8,128)S(1)}, f32[8,256]{1,0:T(8,128)S(1)}, u32[]{:S(2)}, u32[]{:S(2)}) collective-permute-start(f32[8,256]{1,0:T(8,128)S(1)} %broadcast_select_fusion.1), channel_id=1, source_target_pairs={{0,64},{128,192},{1,65},{129,193},{2,66},{130,194},{3,67},{131,195... | collective-permute-start | bytes 24584 | tf_op jit(solution)/shard_map/ppermute | solution.py:223
  13.1 47.4 %all-to-all-start = ((f32[32,8,768]{2,1,0:T(8,128)}), f32[32,8,768]{2,1,0:T(8,128)S(1)}, u32[]{:S(2)}, u32[]{:S(2)}) async-start(f32[32,8,768]{2,1,0:T(8,128)} %broadcast_in_dim.3), calls=%async_computation | async-start | bytes 1572864 | tf_op jit(solution)/shard_map/all_to_all | solution.py:227
  30.6 3.3 %collective-permute-start.3 = (f32[128,512]{1,0:T(8,128)}, f32[128,512]{1,0:T(8,128)S(1)}, u32[]{:S(2)}, u32[]{:S(2)}) collective-permute-start(f32[128,512]{1,0:T(8,128)} %get-tuple-element.24.send), channel_id=1, source_target_pairs={{0,32},{32,0},{1,33},{33,1},{2,34},{34,2},{3,35},{35,3},{4,36},{36... | collective-permute-start | bytes 786440 | tf_op jit(solution)/shard_map/ppermute | solution.py:25
  34.0 0.7 copy-start.1
  36.7 6.6 %collective-permute-start.4 = (f32[32,512]{1,0:T(8,128)}, f32[32,512]{1,0:T(8,128)S(1)}, u32[]{:S(2)}, u32[]{:S(2)}) collective-permute-start(f32[32,512]{1,0:T(8,128)} %get-tuple-element.27), channel_id=1, source_target_pairs={{0,64},{64,128},{128,192},{192,0},{1,65},{65,129},{129,193},{193,1... | collective-permute-start | bytes 196616 | tf_op jit(solution)/shard_map/ppermute | solution.py:21
  38.7 6.9 %collective-permute-start.5 = (f32[32,512]{1,0:T(8,128)}, f32[32,512]{1,0:T(8,128)S(1)}, u32[]{:S(2)}, u32[]{:S(2)}) collective-permute-start(f32[32,512]{1,0:T(8,128)} %get-tuple-element.28), channel_id=1, source_target_pairs={{0,128},{64,192},{128,0},{192,64},{1,129},{65,193},{129,1},{193,65... | collective-permute-start | bytes 196616 | tf_op jit(solution)/shard_map/ppermute | solution.py:21
  42.2 3.6 %collective-permute-start.6 = (f32[32,512]{1,0:T(8,128)}, f32[32,512]{1,0:T(8,128)S(1)}, u32[]{:S(2)}, u32[]{:S(2)}) collective-permute-start(f32[32,512]{1,0:T(8,128)} %get-tuple-element.29), channel_id=1, source_target_pairs={{0,192},{64,0},{128,64},{192,128},{1,193},{65,1},{129,65},{193,129... | collective-permute-start | bytes 196616 | tf_op jit(solution)/shard_map/ppermute | solution.py:21
  43.3 2.5 %copy-start.7 = (f32[32,512]{1,0:T(8,128)}, f32[32,512]{1,0:T(8,128)S(1)}, u32[]{:S(2)}) copy-start(f32[32,512]{1,0:T(8,128)S(1)} %collective-permute-done.4.r1) | copy-start | bytes 196612
  45.6 0.6 copy-start.8
  45.8 0.6 copy-start.9
  48.3 4.5 %collective-permute-start.7 = (f32[32,512]{1,0:T(8,128)}, f32[32,512]{1,0:T(8,128)S(1)}, u32[]{:S(2)}, u32[]{:S(2)}) collective-permute-start(f32[32,512]{1,0:T(8,128)} %get-tuple-element.31), channel_id=1, source_target_pairs={{0,64},{64,128},{128,192},{192,0},{1,65},{65,129},{129,193},{193,1... | collective-permute-start | bytes 196616 | tf_op jit(solution)/shard_map/ppermute | solution.py:21
  49.0 4.9 %collective-permute-start.8 = (f32[32,512]{1,0:T(8,128)}, f32[32,512]{1,0:T(8,128)S(1)}, u32[]{:S(2)}, u32[]{:S(2)}) collective-permute-start(f32[32,512]{1,0:T(8,128)} %get-tuple-element.32), channel_id=1, source_target_pairs={{0,128},{64,192},{128,0},{192,64},{1,129},{65,193},{129,1},{193,65... | collective-permute-start | bytes 196616 | tf_op jit(solution)/shard_map/ppermute | solution.py:21
  51.4 3.6 %collective-permute-start.9 = (f32[32,512]{1,0:T(8,128)}, f32[32,512]{1,0:T(8,128)S(1)}, u32[]{:S(2)}, u32[]{:S(2)}) collective-permute-start(f32[32,512]{1,0:T(8,128)} %get-tuple-element.33), channel_id=1, source_target_pairs={{0,192},{64,0},{128,64},{192,128},{1,193},{65,1},{129,65},{193,129... | collective-permute-start | bytes 196616 | tf_op jit(solution)/shard_map/ppermute | solution.py:21
  52.8 2.2 %copy-start.3 = (f32[32,512]{1,0:T(8,128)}, f32[32,512]{1,0:T(8,128)S(1)}, u32[]{:S(2)}) copy-start(f32[32,512]{1,0:T(8,128)S(1)} %collective-permute-done.7.n1) | copy-start | bytes 196612
  53.9 1.1 %copy-start.4 = (f32[32,512]{1,0:T(8,128)}, f32[32,512]{1,0:T(8,128)S(1)}, u32[]{:S(2)}) copy-start(f32[32,512]{1,0:T(8,128)S(1)} %collective-permute-done.8.n2) | copy-start | bytes 196612
  55.0 0.6 copy-start.5
  57.9 12.8 %collective-permute-start.10 = (f32[128,512]{1,0:T(8,128)}, f32[128,512]{1,0:T(8,128)S(1)}, u32[]{:S(2)}, u32[]{:S(2)}) collective-permute-start(f32[128,512]{1,0:T(8,128)} %get-tuple-element.36), channel_id=1, source_target_pairs={{0,32},{32,0},{1,33},{33,1},{2,34},{34,2},{3,35},{35,3},{4,36},{36... | collective-permute-start | bytes 786440 | tf_op jit(solution)/shard_map/ppermute | solution.py:25
  60.5 0.9 %copy-start = (f32[32,8,768]{2,1,0:T(8,128)}, f32[32,8,768]{2,1,0:T(8,128)S(1)}, u32[]{:S(2)}) copy-start(f32[32,8,768]{2,1,0:T(8,128)S(1)} %all-to-all-done) | copy-start | bytes 2359300
  70.7 0.7 copy-start.2

commit v2 on v1

v2 whole, which is shorter than its diff:
```python
import jax
import jax.numpy as jnp
from jax import lax
from jax.experimental import pallas as pl
from jax.experimental.pallas import tpu as pltpu
from jax.sharding import Mesh
from jax.sharding import PartitionSpec as P

ROW = ("x", "core")
COL = ("y", "z")
PARAMS = pltpu.CompilerParams(vmem_limit_bytes=12 * 1024 * 1024)
VMEM = pl.BlockSpec(memory_space=pltpu.VMEM)
SMEM = pl.BlockSpec(memory_space=pltpu.SMEM)


def f32(*shape):
    return jax.ShapeDtypeStruct(shape, jnp.float32)


def chip_shift(value, step):
    return lax.ppermute(value, "x", [(i, (i + step) % 4) for i in range(4)])


def split(value):
    high = value.astype(jnp.bfloat16)
    return high, (value - high.astype(jnp.float32)).astype(jnp.bfloat16)


def product(left, right):
    def dot(a, b):
        return jnp.dot(a, b, preferred_element_type=jnp.float32)

    return dot(left[0], right[0]) + (dot(left[0], right[1]) + dot(left[1], right[0]))


def core_swap(value):
    return lax.ppermute(value, "core", [(0, 1), (1, 0)])


def plan_kernel(piv, where_am_i, t_ref, keep, send, meta, places, order, picks):
    width = piv.shape[0]
    half = width // 2
    rows = t_ref.shape[0]
    shift = rows.bit_length() - 1
    chip, core = where_am_i[0], where_am_i[1]
    device = chip * 2 + core
    first = device * rows

    def init(j, carry):
        p = piv[j]
        order[p] = p
        order[j] = j
        return carry

    lax.fori_loop(0, width, init, 0, unroll=16)

    def swap(j, carry):
        p = piv[j]
        a = order[j]
        b = order[p]
        order[j] = b
        order[p] = a
        return carry

    lax.fori_loop(0, width, swap, 0, unroll=16)

    def pick(slot, count):
        src = order[slot]
        down = order[src]
        local = src - first
        own = (local >= 0) & (local < rows)
        picks[slot] = jnp.where(own, local, jnp.where(device == 0, down, 0))
        picks[width + slot] = lax.shift_right_logical(src, shift)
        places[1 + count] = slot
        places[1 + width + count] = local
        places[1 + 2 * width + count] = down
        return count + jnp.where(own & (src >= width), 1, 0)

    places[0] = lax.fori_loop(0, width, pick, 0, unroll=8)

    def gather(i, carry):
        for base, out in ((core * half, keep), ((1 - core) * half, send)):
            slot = base + i
            out[pl.ds(i, 1), :] = t_ref[pl.ds(picks[slot], 1), :]
            meta[pl.ds(slot, 1), :] = jnp.full((1, 128), picks[width + slot], jnp.int32)
        return carry

    lax.fori_loop(0, half, gather, 0, unroll=8)


def owner_of(device, columns):
    device = jnp.concatenate([device] * (columns // 128), axis=1)
    return lax.shift_right_logical(device, 1), device & 1


def combine_kernel(where_am_i, keep, got, meta, joined, p1, p2, p3):
    chip, core = where_am_i[0], where_am_i[1]
    half = keep.shape[0]
    part = half // 4
    owner_chip, owner_core = owner_of(meta[pl.ds(core * half, half), :], keep.shape[1])
    mine = owner_chip == chip
    other = (mine & (owner_core != core)) | (~mine & ((chip == 0) & (core == 1)))
    joined[...] = jnp.where(other, got[...], keep[...])
    for step, out in ((1, p1), (2, p2), (3, p3)):
        out[...] = joined[pl.ds(lax.rem(chip + step, 4) * part, part), :]


def route_kernel(where_am_i, joined, r1, r2, r3, meta, m0, m1, m2, m3):
    chip, core = where_am_i[0], where_am_i[1]
    half = joined.shape[0]
    part = half // 4
    owner_chip, _ = owner_of(
        meta[pl.ds(core * half + chip * part, part), :], joined.shape[1]
    )
    own = joined[pl.ds(chip * part, part), :]
    a, b, c = r1[...], r2[...], r3[...]
    behind = (chip - owner_chip) & 3
    pivot_row = jnp.where(
        behind == 0, own, jnp.where(behind == 1, a, jnp.where(behind == 2, b, c))
    )
    top_row = jnp.where(
        chip == 0, own, jnp.where(chip == 1, a, jnp.where(chip == 2, b, c))
    )
    for step, out in enumerate((m0, m1, m2, m3)):
        out[...] = jnp.where(
            owner_chip == lax.rem(chip + step, 4), top_row, pivot_row
        )


def halves_kernel(
    where_am_i, n0, n1, n2, n3, joined, keep, got, meta, message, pivot_half, top_half, g
):
    chip, core = where_am_i[0], where_am_i[1]
    half = joined.shape[0]
    part = half // 4
    for step, src in enumerate((n0, n1, n2, n3)):
        g[pl.ds(lax.rem(chip - step + 4, 4) * part, part), :] = src[...]
    owner_chip, owner_core = owner_of(meta[pl.ds(core * half, half), :], joined.shape[1])
    mine = owner_chip == chip
    routed = g[...]
    rows = joined[...]
    pivot_half[...] = jnp.where(mine, rows, routed)
    first_device = (chip == 0) & (core == 0)
    message[...] = jnp.where(
        mine & first_device,
        keep[...],
        jnp.where(mine & (owner_core == core), rows, routed),
    )
    top_half[...] = jnp.where(chip == 0, got[...], routed)


def final_kernel(
    where_am_i, places, t_ref, wh_ref, wl_ref, pivot_half, top_half, send, got, meta, out, pivot
):
    chip, core = where_am_i[0], where_am_i[1]
    rows = t_ref.shape[0]
    half = pivot_half.shape[0]
    width = 2 * half
    device = chip * 2 + core
    owner_chip, owner_core = owner_of(
        meta[pl.ds((1 - core) * half, half), :], got.shape[1]
    )
    here = (owner_chip == chip) & (owner_core == core)
    pivot[pl.ds(core * half, half), :] = pivot_half[...]
    pivot[pl.ds((1 - core) * half, half), :] = jnp.where(here, send[...], got[...])
    out[...] = t_ref[...]

    def place(i, carry):
        slot = places[1 + i]
        target = pl.ds(places[1 + width + i], 1)
        in_half = (slot >= half) == (core == 1)
        index = slot & (half - 1)
        late = jnp.where(in_half, 1, 0)
        row = jnp.where(
            device == 0,
            t_ref[pl.ds(jnp.where(device == 0, places[1 + 2 * width + i], 0), 1), :],
            jnp.where(
                late == 1, top_half[pl.ds(index, 1), :], got[pl.ds(index, 1), :]
            ),
        )
        out[target, :] = row
        return carry

    lax.fori_loop(0, places[0], place, 0)

    @pl.when(device == 0)
    def _():
        out[0:width, :] = jnp.zeros((width, out.shape[1]), jnp.float32)

    weights = wh_ref[...], wl_ref[...]
    out[...] -= product(weights, split(pivot[...]))


def weights_kernel(where_am_i, stacked, wh_ref, wl_ref):
    width = stacked.shape[0]
    rows = stacked.shape[1] - width
    square = stacked[:, rows:]
    row = lax.broadcasted_iota(jnp.int32, (width, width), 0)
    col = lax.broadcasted_iota(jnp.int32, (width, width), 1)
    apart = row ^ col
    inv = jnp.where(row == col, 1.0, 0.0)
    level = 0
    while (1 << level) < width:
        size = 1 << level
        link = (lax.shift_right_logical(apart, level) == 1) & ((col & size) != 0)
        off = jnp.where(link, square, 0.0)
        if level == 0:
            inv = inv - off
        else:
            parts = split(inv)
            inv = inv - product(split(product(parts, split(off))), parts)
        level += 1
    weights = product(split(inv), split(stacked[:, :rows])).T
    high, low = split(weights)
    wh_ref[...] = high
    wl_ref[...] = low

    @pl.when((where_am_i[0] == 0) & (where_am_i[1] == 0))
    def _():
        high, low = split(-inv.T)
        wh_ref[0:width, :] = high
        wl_ref[0:width, :] = low


def on_device(trailing, panel_factors, pivots):
    rows, columns = trailing.shape
    width = pivots.shape[0]
    half, part = width // 2, width // 8
    chip, core = lax.axis_index("x"), lax.axis_index("core")
    here = jnp.stack([chip, core]).astype(jnp.int32)

    panel = panel_factors.T
    square = panel[:, :width]
    square = jnp.where(core == 1, lax.ppermute(square, "core", [(0, 1)]), square)
    square = jnp.where(chip == 2, lax.ppermute(square, "x", [(0, 2)]), square)
    square = jnp.where(
        chip % 2 == 1, lax.ppermute(square, "x", [(0, 1), (2, 3)]), square
    )
    block = jnp.concatenate([panel, square], axis=1)
    copies = jnp.broadcast_to(block, (lax.axis_size(COL), *block.shape))
    stacked = lax.all_to_all(copies, COL, split_axis=0, concat_axis=0, tiled=True)
    stacked = stacked.reshape(width, rows + width)
    half_weights = jax.ShapeDtypeStruct((rows, width), jnp.bfloat16)
    high, low = pl.pallas_call(
        weights_kernel,
        out_shape=(half_weights, half_weights),
        in_specs=[SMEM, VMEM],
        out_specs=(VMEM, VMEM),
        compiler_params=PARAMS,
    )(here, stacked)

    keep, send, meta, places = pl.pallas_call(
        plan_kernel,
        out_shape=(
            f32(half, columns),
            f32(half, columns),
            jax.ShapeDtypeStruct((width, 128), jnp.int32),
            jax.ShapeDtypeStruct((1024,), jnp.int32),
        ),
        in_specs=[SMEM, SMEM, VMEM],
        out_specs=(VMEM, VMEM, VMEM, SMEM),
        scratch_shapes=[
            pltpu.SMEM((rows * 8,), jnp.int32),
            pltpu.SMEM((2 * width,), jnp.int32),
        ],
        compiler_params=PARAMS,
    )(pivots, here, trailing)
    got = core_swap(send)
    joined, p1, p2, p3 = pl.pallas_call(
        combine_kernel,
        out_shape=(f32(half, columns),) + (f32(part, columns),) * 3,
        in_specs=[SMEM, VMEM, VMEM, VMEM],
        out_specs=(VMEM,) * 4,
        compiler_params=PARAMS,
    )(here, keep, got, meta)
    r1, r2, r3 = (chip_shift(p, s) for s, p in ((1, p1), (2, p2), (3, p3)))
    m0, m1, m2, m3 = pl.pallas_call(
        route_kernel,
        out_shape=(f32(part, columns),) * 4,
        in_specs=[SMEM] + [VMEM] * 5,
        out_specs=(VMEM,) * 4,
        compiler_params=PARAMS,
    )(here, joined, r1, r2, r3, meta)
    n1, n2, n3 = (chip_shift(m, s) for s, m in ((1, m1), (2, m2), (3, m3)))
    message, pivot_half, top_half = pl.pallas_call(
        halves_kernel,
        out_shape=(f32(half, columns),) * 3,
        in_specs=[SMEM] + [VMEM] * 8,
        out_specs=(VMEM,) * 3,
        scratch_shapes=[pltpu.VMEM((half, columns), jnp.float32)],
        compiler_params=PARAMS,
    )(here, m0, n1, n2, n3, joined, keep, got, meta)
    last = core_swap(message)
    return pl.pallas_call(
        final_kernel,
        out_shape=f32(rows, columns),
        in_specs=[SMEM, SMEM] + [VMEM] * 8,
        out_specs=VMEM,
        scratch_shapes=[pltpu.VMEM((width, columns), jnp.float32)],
        compiler_params=PARAMS,
    )(here, places, trailing, high, low, pivot_half, top_half, send, last, meta)


def solution(mesh):
    torus = Mesh(mesh.devices.reshape(4, 2, 4, 8), ("x", "core", "y", "z"))
    return jax.shard_map(
        on_device,
        mesh=torus,
        in_specs=(P(ROW, COL), P(ROW, COL), P()),
        out_specs=P(ROW, COL),
        check_vma=False,
    )
```

time: 79.3 us -> 62.1 us (0.78)
  Pallas kernels: 28.6 us -> 15.5 us
  local copies, waits for them, and re-layouts: 5.23 us -> 2.3 us
    pallas_call x1, Pallas kernels: 7.44 us -> 2.86 us  [on_device(): pl.pallas_call(final_kernel, out_shape=f32(rows, columns), in_specs=[SMEM...]
    pallas_call x1, Pallas kernels: 9.29 us -> 4.72 us  [on_device(): pl.pallas_call(weights_kernel, out_shape=(half_weights, half_weights), in...]
    unnamed x20 -> x6, local copies, waits for them, and re-layouts: 3.52 us -> 0.6 us
    pallas_call x1, Pallas kernels: 2.33 us -> 0.71 us  [on_device(): pl.pallas_call(halves_kernel, out_shape=(f32(half, columns),) * 3, in_spe...]
    pallas_call x1, Pallas kernels: 2.01 us -> 0.62 us  [on_device(): pl.pallas_call(combine_kernel, out_shape=(f32(half, columns),) + (f32(par...]
    pallas_call x1, Pallas kernels: 1.86 us -> 0.58 us  [on_device(): pl.pallas_call(route_kernel, out_shape=(f32(part, columns),) * 4, in_spec...]
  transfers between devices with their start and end apart: 12 -> 12, of which waited for: 10 -> 10; matrix products, arithmetic and copies ran while one was open for 1% -> 0% of each run, Pallas kernels for 27% -> 20%
where the time goes in v2:
time: 62.1 us; the launch traced here: 61.8 us
  starting transfers between devices  31 us (50%)
  Pallas kernels  15.5 us (25%)
  waiting for transfers between devices  12.8 us (21%)
  local copies, waits for them, and re-layouts  2.3 us (4%)
    all_to_all x1, starting transfers between devices, on_device(): lax.all_to_all(copies, COL, split_axis=0, concat_axis=0, tiled=True)  11.2 us
    ppermute x6, starting transfers between devices, chip_shift(): return lax.ppermute(value, 'x', [(i, (i + step) % 4) for i in range(4)])  9.32 us
    ppermute x6, waiting for transfers between devices, chip_shift(): return lax.ppermute(value, 'x', [(i, (i + step) % 4) for i in range(4)])  6.31 us
    pallas_call x1, Pallas kernels, on_device(): pl.pallas_call(plan_kernel, out_shape=(f32(half, columns), f32(half, colu...  5.97 us
    pallas_call x1, Pallas kernels, on_device(): pl.pallas_call(weights_kernel, out_shape=(half_weights, half_weights), in...  4.72 us
    ppermute x2, starting transfers between devices, core_swap(): return lax.ppermute(value, 'core', [(0, 1), (1, 0)])  4.57 us
    ppermute x1, waiting for transfers between devices, on_device(): lax.ppermute(square, 'core', [(0, 1)])  3.84 us
    ppermute x1, starting transfers between devices, on_device(): square = jnp.where(chip == 2, lax.ppermute(square, 'x', [(0, 2)]), square)  3.38 us
  transfers between devices with their start and end apart: 12, of which 10 were waited for; matrix products, arithmetic and copies ran while one was open for 0% of the time, Pallas kernels for 20%

profile of v2, /device:TPU:1, one launch (start us, length us, event | category | flops | bytes accessed | tf_op | source)
XLA Modules:
  0.0 61.8 jit_solution(5883692275078475948)
XLA Ops:
  0.0 0.8 %slice.4 = f32[8,256]{1,0:T(8,128)S(1)} slice(f32[8,512]{1,0:T(8,128)} %bitcast.5), slice={[0:8], [0:256]} | slice | bytes 16384 | tf_op jit(solution)/shard_map/slice | solution.py:233
  0.8 1.3 %collective-permute-start = (f32[8,256]{1,0:T(8,128)S(1)}, f32[8,256]{1,0:T(8,128)S(1)}, u32[]{:S(2)}, u32[]{:S(2)}) collective-permute-start(f32[8,256]{1,0:T(8,128)S(1)} %slice.4), channel_id=1, source_target_pairs={{0,32},{1,33},{2,34},{3,35},{4,36},{5,37},{6,38},{7,39},{8,40},{9,... | collective-permute-start | bytes 24584 | tf_op jit(solution)/shard_map/ppermute | solution.py:234
  2.1 3.8 %collective-permute-done = f32[8,256]{1,0:T(8,128)S(1)} collective-permute-done((f32[8,256]{1,0:T(8,128)S(1)}, f32[8,256]{1,0:T(8,128)S(1)}, u32[]{:S(2)}, u32[]{:S(2)}) %collective-permute-start) | collective-permute-done | bytes 8224 | tf_op jit(solution)/shard_map/ppermute | solution.py:234
  5.9 3.4 %collective-permute-start.1 = (f32[8,256]{1,0:T(8,128)S(1)}, f32[8,256]{1,0:T(8,128)S(1)}, u32[]{:S(2)}, u32[]{:S(2)}) collective-permute-start(f32[8,256]{1,0:T(8,128)S(1)} %broadcast_select_fusion), channel_id=1, source_target_pairs={{0,128},{1,129},{2,130},{3,131},{4,132},{5,133},{6,134},{7,135},{8... | collective-permute-start | bytes 24584 | tf_op jit(solution)/shard_map/ppermute | solution.py:235
  9.3 0.8 %collective-permute-done.1 = f32[8,256]{1,0:T(8,128)S(1)} collective-permute-done((f32[8,256]{1,0:T(8,128)S(1)}, f32[8,256]{1,0:T(8,128)S(1)}, u32[]{:S(2)}, u32[]{:S(2)}) %collective-permute-start.1) | collective-permute-done | bytes 8224 | tf_op jit(solution)/shard_map/ppermute | solution.py:235
  10.1 1.3 %collective-permute-start.2 = (f32[8,256]{1,0:T(8,128)S(1)}, f32[8,256]{1,0:T(8,128)S(1)}, u32[]{:S(2)}, u32[]{:S(2)}) collective-permute-start(f32[8,256]{1,0:T(8,128)S(1)} %broadcast_select_fusion.1), channel_id=1, source_target_pairs={{0,64},{128,192},{1,65},{129,193},{2,66},{130,194},{3,67},{131,195... | collective-permute-start | bytes 24584 | tf_op jit(solution)/shard_map/ppermute | solution.py:237
  11.4 0.8 %collective-permute-done.2 = f32[8,256]{1,0:T(8,128)S(1)} collective-permute-done((f32[8,256]{1,0:T(8,128)S(1)}, f32[8,256]{1,0:T(8,128)S(1)}, u32[]{:S(2)}, u32[]{:S(2)}) %collective-permute-start.2) | collective-permute-done | bytes 8224 | tf_op jit(solution)/shard_map/ppermute | solution.py:237
  12.2 0.9 %broadcast_in_dim.3 = f32[32,8,768]{2,1,0:T(8,128)} broadcast(f32[8,768]{1,0:T(8,128)S(1)} %pad_maximum_fusion), dimensions={1,2} | broadcast | bytes 811008 | tf_op jit(solution)/shard_map/broadcast_in_dim | solution.py:240
  13.1 11.2 %all-to-all-start = ((f32[32,8,768]{2,1,0:T(8,128)}), f32[32,8,768]{2,1,0:T(8,128)S(1)}, u32[]{:S(2)}, u32[]{:S(2)}) async-start(f32[32,8,768]{2,1,0:T(8,128)} %broadcast_in_dim.3), calls=%async_computation | async-start | bytes 1572864 | tf_op jit(solution)/shard_map/all_to_all | solution.py:241
  25.0 6.0 %shard_map.37 = (f32[128,512]{1,0:T(8,128)S(1)}, f32[128,512]{1,0:T(8,128)S(1)}, s32[256,128]{1,0:T(8,128)S(1)}, s32[1024]{0:T(1024)S(1)}) custom-call(s32[256]{0:T(256)S(1)} %copy-done.1, s32[2]{0:T(128)S(1)} %pad_add_fusion.where_am_i, f32[512,512]{1,0:T(8,128)S(1)} %copy-done), custom_call_target="tpu_custom_call" | custom-call | tf_op jit(solution)/shard_map/pallas_call | solution.py:252
  31.0 2.0 %collective-permute-start.3 = (f32[128,512]{1,0:T(8,128)S(1)}, f32[128,512]{1,0:T(8,128)S(1)}, u32[]{:S(2)}, u32[]{:S(2)}) collective-permute-start(f32[128,512]{1,0:T(8,128)S(1)} %get-tuple-element.26.send), channel_id=1, source_target_pairs={{0,32},{32,0},{1,33},{33,1},{2,34},{34,2},{3,35},{35,3},{4,36},{36... | collective-permute-start | bytes 786440 | tf_op jit(solution)/shard_map/ppermute | solution.py:37
  32.9 1.2 %collective-permute-done.3.got = f32[128,512]{1,0:T(8,128)S(1)} collective-permute-done((f32[128,512]{1,0:T(8,128)S(1)}, f32[128,512]{1,0:T(8,128)S(1)}, u32[]{:S(2)}, u32[]{:S(2)}) %collective-permute-start.3) | collective-permute-done | bytes 262176 | tf_op jit(solution)/shard_map/ppermute | solution.py:37
  34.7 2.1 %collective-permute-start.4 = (f32[32,512]{1,0:T(8,128)S(1)}, f32[32,512]{1,0:T(8,128)S(1)}, u32[]{:S(2)}, u32[]{:S(2)}) collective-permute-start(f32[32,512]{1,0:T(8,128)S(1)} %get-tuple-element.29), channel_id=1, source_target_pairs={{0,64},{64,128},{128,192},{192,0},{1,65},{65,129},{129,193},{193,1... | collective-permute-start | bytes 196616 | tf_op jit(solution)/shard_map/ppermute | solution.py:21
  36.8 3.5 %collective-permute-start.5 = (f32[32,512]{1,0:T(8,128)S(1)}, f32[32,512]{1,0:T(8,128)S(1)}, u32[]{:S(2)}, u32[]{:S(2)}) collective-permute-start(f32[32,512]{1,0:T(8,128)S(1)} %get-tuple-element.30), channel_id=1, source_target_pairs={{0,128},{64,192},{128,0},{192,64},{1,129},{65,193},{129,1},{193,65... | collective-permute-start | bytes 196616 | tf_op jit(solution)/shard_map/ppermute | solution.py:21
  40.4 0.8 %collective-permute-done.4.r1 = f32[32,512]{1,0:T(8,128)S(1)} collective-permute-done((f32[32,512]{1,0:T(8,128)S(1)}, f32[32,512]{1,0:T(8,128)S(1)}, u32[]{:S(2)}, u32[]{:S(2)}) %collective-permute-start.4) | collective-permute-done | bytes 65568 | tf_op jit(solution)/shard_map/ppermute | solution.py:21
  41.2 2.3 %collective-permute-done.5.r2 = f32[32,512]{1,0:T(8,128)S(1)} collective-permute-done((f32[32,512]{1,0:T(8,128)S(1)}, f32[32,512]{1,0:T(8,128)S(1)}, u32[]{:S(2)}, u32[]{:S(2)}) %collective-permute-start.5) | collective-permute-done | bytes 65568 | tf_op jit(solution)/shard_map/ppermute | solution.py:21
  44.3 0.8 %collective-permute-start.7 = (f32[32,512]{1,0:T(8,128)S(1)}, f32[32,512]{1,0:T(8,128)S(1)}, u32[]{:S(2)}, u32[]{:S(2)}) collective-permute-start(f32[32,512]{1,0:T(8,128)S(1)} %get-tuple-element.33), channel_id=1, source_target_pairs={{0,64},{64,128},{128,192},{192,0},{1,65},{65,129},{129,193},{193,1... | collective-permute-start | bytes 196616 | tf_op jit(solution)/shard_map/ppermute | solution.py:21
  45.1 2.4 %collective-permute-start.8 = (f32[32,512]{1,0:T(8,128)S(1)}, f32[32,512]{1,0:T(8,128)S(1)}, u32[]{:S(2)}, u32[]{:S(2)}) collective-permute-start(f32[32,512]{1,0:T(8,128)S(1)} %get-tuple-element.34), channel_id=1, source_target_pairs={{0,128},{64,192},{128,0},{192,64},{1,129},{65,193},{129,1},{193,65... | collective-permute-start | bytes 196616 | tf_op jit(solution)/shard_map/ppermute | solution.py:21
  48.0 0.7 %collective-permute-done.7.n1 = f32[32,512]{1,0:T(8,128)S(1)} collective-permute-done((f32[32,512]{1,0:T(8,128)S(1)}, f32[32,512]{1,0:T(8,128)S(1)}, u32[]{:S(2)}, u32[]{:S(2)}) %collective-permute-start.7) | collective-permute-done | bytes 65568 | tf_op jit(solution)/shard_map/ppermute | solution.py:21
  48.7 1.2 %collective-permute-done.8.n2 = f32[32,512]{1,0:T(8,128)S(1)} collective-permute-done((f32[32,512]{1,0:T(8,128)S(1)}, f32[32,512]{1,0:T(8,128)S(1)}, u32[]{:S(2)}, u32[]{:S(2)}) %collective-permute-start.8) | collective-permute-done | bytes 65568 | tf_op jit(solution)/shard_map/ppermute | solution.py:21
  49.9 1.1 %collective-permute-done.9.n3 = f32[32,512]{1,0:T(8,128)S(1)} collective-permute-done((f32[32,512]{1,0:T(8,128)S(1)}, f32[32,512]{1,0:T(8,128)S(1)}, u32[]{:S(2)}, u32[]{:S(2)}) %collective-permute-start.9) | collective-permute-done | bytes 65568 | tf_op jit(solution)/shard_map/ppermute | solution.py:21
  51.6 2.6 %collective-permute-start.10 = (f32[128,512]{1,0:T(8,128)S(1)}, f32[128,512]{1,0:T(8,128)S(1)}, u32[]{:S(2)}, u32[]{:S(2)}) collective-permute-start(f32[128,512]{1,0:T(8,128)S(1)} %get-tuple-element.38), channel_id=1, source_target_pairs={{0,32},{32,0},{1,33},{33,1},{2,34},{34,2},{3,35},{35,3},{4,36},{36... | collective-permute-start | bytes 786440 | tf_op jit(solution)/shard_map/ppermute | solution.py:37
  54.3 4.7 %shard_map.38 = (bf16[512,256]{1,0:T(8,128)(2,1)S(1)}, bf16[512,256]{1,0:T(8,128)(2,1)S(1)}) custom-call(s32[2]{0:T(128)S(1)} %pad_add_fusion.where_am_i, f32[256,768]{1,0:T(8,128)S(1)} %bitcast.4), custom_call_target="tpu_custom_call" | custom-call | tf_op jit(solution)/shard_map/pallas_call | solution.py:244
  59.0 2.9 %shard_map.42 = f32[512,512]{1,0:T(8,128)} custom-call(s32[2]{0:T(128)S(1)} %pad_add_fusion.where_am_i, s32[1024]{0:T(1024)S(1)} %get-tuple-element.22.places, f32[512,512]{1,0:T(8,128)S(1)} %copy-done, bf16[512,256]{1,0:T(8,128)(2,1)S(1)} %get-tuple-element.23.wh_ref, bf16[512,256]{1,0:T(8,128)(2,1)S(1)} %get-tuple-element.24.wl_ref, ...), custom_call_target="tpu_custom_call" | custom-call | tf_op jit(solution)/shard_map/pallas_call | solution.py:294
  (19 shorter events, 3.3 us)
Async XLA Ops:
  0.0 5.9 %copy-start.2 = (f32[512,8]{0,1:T(8,128)S(1)}, f32[512,8]{0,1:T(8,128)}, u32[]{:S(2)}) copy-start(f32[512,8]{0,1:T(8,128)} %param.4) | copy-start | bytes 49156
  0.8 5.1 %collective-permute-start = (f32[8,256]{1,0:T(8,128)S(1)}, f32[8,256]{1,0:T(8,128)S(1)}, u32[]{:S(2)}, u32[]{:S(2)}) collective-permute-start(f32[8,256]{1,0:T(8,128)S(1)} %slice.4), channel_id=1, source_target_pairs={{0,32},{1,33},{2,34},{3,35},{4,36},{5,37},{6,38},{7,39},{8,40},{9,... | collective-permute-start | bytes 24584 | tf_op jit(solution)/shard_map/ppermute | solution.py:234
  5.9 4.2 %collective-permute-start.1 = (f32[8,256]{1,0:T(8,128)S(1)}, f32[8,256]{1,0:T(8,128)S(1)}, u32[]{:S(2)}, u32[]{:S(2)}) collective-permute-start(f32[8,256]{1,0:T(8,128)S(1)} %broadcast_select_fusion), channel_id=1, source_target_pairs={{0,128},{1,129},{2,130},{3,131},{4,132},{5,133},{6,134},{7,135},{8... | collective-permute-start | bytes 24584 | tf_op jit(solution)/shard_map/ppermute | solution.py:235
  10.1 2.1 %collective-permute-start.2 = (f32[8,256]{1,0:T(8,128)S(1)}, f32[8,256]{1,0:T(8,128)S(1)}, u32[]{:S(2)}, u32[]{:S(2)}) collective-permute-start(f32[8,256]{1,0:T(8,128)S(1)} %broadcast_select_fusion.1), channel_id=1, source_target_pairs={{0,64},{128,192},{1,65},{129,193},{2,66},{130,194},{3,67},{131,195... | collective-permute-start | bytes 24584 | tf_op jit(solution)/shard_map/ppermute | solution.py:237
  12.1 12.2 %copy-start = (f32[512,512]{1,0:T(8,128)S(1)}, f32[512,512]{1,0:T(8,128)}, u32[]{:S(2)}) copy-start(f32[512,512]{1,0:T(8,128)} %t_ref.3) | copy-start | bytes 3145732
  13.1 41.2 %all-to-all-start = ((f32[32,8,768]{2,1,0:T(8,128)}), f32[32,8,768]{2,1,0:T(8,128)S(1)}, u32[]{:S(2)}, u32[]{:S(2)}) async-start(f32[32,8,768]{2,1,0:T(8,128)} %broadcast_in_dim.3), calls=%async_computation | async-start | bytes 1572864 | tf_op jit(solution)/shard_map/all_to_all | solution.py:241
  24.3 0.7 %copy-start.1 = (s32[256]{0:T(256)S(1)}, s32[256]{0:T(256)}, u32[]{:S(2)}) copy-start(s32[256]{0:T(256)} %piv.1) | copy-start | bytes 3076
  31.0 3.1 %collective-permute-start.3 = (f32[128,512]{1,0:T(8,128)S(1)}, f32[128,512]{1,0:T(8,128)S(1)}, u32[]{:S(2)}, u32[]{:S(2)}) collective-permute-start(f32[128,512]{1,0:T(8,128)S(1)} %get-tuple-element.26.send), channel_id=1, source_target_pairs={{0,32},{32,0},{1,33},{33,1},{2,34},{34,2},{3,35},{35,3},{4,36},{36... | collective-permute-start | bytes 786440 | tf_op jit(solution)/shard_map/ppermute | solution.py:37
  34.7 6.5 %collective-permute-start.4 = (f32[32,512]{1,0:T(8,128)S(1)}, f32[32,512]{1,0:T(8,128)S(1)}, u32[]{:S(2)}, u32[]{:S(2)}) collective-permute-start(f32[32,512]{1,0:T(8,128)S(1)} %get-tuple-element.29), channel_id=1, source_target_pairs={{0,64},{64,128},{128,192},{192,0},{1,65},{65,129},{129,193},{193,1... | collective-permute-start | bytes 196616 | tf_op jit(solution)/shard_map/ppermute | solution.py:21
  36.8 6.7 %collective-permute-start.5 = (f32[32,512]{1,0:T(8,128)S(1)}, f32[32,512]{1,0:T(8,128)S(1)}, u32[]{:S(2)}, u32[]{:S(2)}) collective-permute-start(f32[32,512]{1,0:T(8,128)S(1)} %get-tuple-element.30), channel_id=1, source_target_pairs={{0,128},{64,192},{128,0},{192,64},{1,129},{65,193},{129,1},{193,65... | collective-permute-start | bytes 196616 | tf_op jit(solution)/shard_map/ppermute | solution.py:21
  40.3 3.4 %collective-permute-start.6 = (f32[32,512]{1,0:T(8,128)S(1)}, f32[32,512]{1,0:T(8,128)S(1)}, u32[]{:S(2)}, u32[]{:S(2)}) collective-permute-start(f32[32,512]{1,0:T(8,128)S(1)} %get-tuple-element.31), channel_id=1, source_target_pairs={{0,192},{64,0},{128,64},{192,128},{1,193},{65,1},{129,65},{193,129... | collective-permute-start | bytes 196616 | tf_op jit(solution)/shard_map/ppermute | solution.py:21
  44.3 4.4 %collective-permute-start.7 = (f32[32,512]{1,0:T(8,128)S(1)}, f32[32,512]{1,0:T(8,128)S(1)}, u32[]{:S(2)}, u32[]{:S(2)}) collective-permute-start(f32[32,512]{1,0:T(8,128)S(1)} %get-tuple-element.33), channel_id=1, source_target_pairs={{0,64},{64,128},{128,192},{192,0},{1,65},{65,129},{129,193},{193,1... | collective-permute-start | bytes 196616 | tf_op jit(solution)/shard_map/ppermute | solution.py:21
  45.1 4.8 %collective-permute-start.8 = (f32[32,512]{1,0:T(8,128)S(1)}, f32[32,512]{1,0:T(8,128)S(1)}, u32[]{:S(2)}, u32[]{:S(2)}) collective-permute-start(f32[32,512]{1,0:T(8,128)S(1)} %get-tuple-element.34), channel_id=1, source_target_pairs={{0,128},{64,192},{128,0},{192,64},{1,129},{65,193},{129,1},{193,65... | collective-permute-start | bytes 196616 | tf_op jit(solution)/shard_map/ppermute | solution.py:21
  47.5 3.4 %collective-permute-start.9 = (f32[32,512]{1,0:T(8,128)S(1)}, f32[32,512]{1,0:T(8,128)S(1)}, u32[]{:S(2)}, u32[]{:S(2)}) collective-permute-start(f32[32,512]{1,0:T(8,128)S(1)} %get-tuple-element.35), channel_id=1, source_target_pairs={{0,192},{64,0},{128,64},{192,128},{1,193},{65,1},{129,65},{193,129... | collective-permute-start | bytes 196616 | tf_op jit(solution)/shard_map/ppermute | solution.py:21
  51.6 7.3 %collective-permute-start.10 = (f32[128,512]{1,0:T(8,128)S(1)}, f32[128,512]{1,0:T(8,128)S(1)}, u32[]{:S(2)}, u32[]{:S(2)}) collective-permute-start(f32[128,512]{1,0:T(8,128)S(1)} %get-tuple-element.38), channel_id=1, source_target_pairs={{0,32},{32,0},{1,33},{33,1},{2,34},{34,2},{3,35},{35,3},{4,36},{36... | collective-permute-start | bytes 786440 | tf_op jit(solution)/shard_map/ppermute | solution.py:37

commit v3 on v2

v3 whole, which is shorter than its diff:
```python
import jax
import jax.numpy as jnp
from jax import lax
from jax.experimental import pallas as pl
from jax.experimental.pallas import tpu as pltpu
from jax.sharding import Mesh
from jax.sharding import PartitionSpec as P


ROW = ("x", "core")
COL = ("y", "z")
PARAMS = pltpu.CompilerParams(vmem_limit_bytes=12 * 1024 * 1024)
VMEM = pl.BlockSpec(memory_space=pltpu.VMEM)
SMEM = pl.BlockSpec(memory_space=pltpu.SMEM)


def f32(*shape):
    return jax.ShapeDtypeStruct(shape, jnp.float32)


def along(value, axis, step):
    size = lax.axis_size(axis)
    return lax.ppermute(value, axis, [(i, (i + step) % size) for i in range(size)])


def swapped(value, axis, bit):
    return lax.ppermute(value, axis, [(i, i ^ bit) for i in range(lax.axis_size(axis))])


def split(value):
    high = value.astype(jnp.bfloat16)
    return high, (value - high.astype(jnp.float32)).astype(jnp.bfloat16)


def product(left, right):
    def dot(a, b):
        return jnp.dot(a, b, preferred_element_type=jnp.float32)

    return dot(left[0], right[0]) + (dot(left[0], right[1]) + dot(left[1], right[0]))


def plan_kernel(piv, where_am_i, t_hbm, keep, send, meta, places, order, picks, t_ref, arrived):
    fetch = pltpu.make_async_copy(t_hbm, t_ref, arrived)
    fetch.start()
    width = piv.shape[0]
    half = width // 2
    rows = t_ref.shape[0]
    shift = rows.bit_length() - 1
    chip, core = where_am_i[0], where_am_i[1]
    device = chip * 2 + core

    def init(j, carry):
        p = piv[j]
        order[p] = p
        order[j] = j
        return carry

    lax.fori_loop(0, width, init, 0, unroll=16)

    def swap(j, carry):
        p = piv[j]
        a = order[j]
        b = order[p]
        order[j] = b
        order[p] = a
        return carry

    lax.fori_loop(0, width, swap, 0, unroll=16)

    def pick(slot, count):
        src = order[slot]
        down = order[src]
        local = src & (rows - 1)
        own = lax.shift_right_logical(src, shift) == device
        picks[slot] = jnp.where(own, local, down & (rows - 1))
        places[1 + count] = slot | (local << 8) | (down << 20)
        return count + jnp.where(own & (src >= width), 1, 0)

    places[0] = lax.fori_loop(0, width, pick, 0, unroll=8)

    def gather(group, carry):
        for base, out in ((core * half, keep), ((1 - core) * half, send)):
            for k in range(8):
                start = pl.multiple_of(group * 8, 8)
                slot = base + start + k
                out[pl.ds(start + k, 1), :] = t_ref[pl.ds(picks[slot], 1), :]
                owner = lax.shift_right_logical(order[slot], shift)
                meta[pl.ds(pl.multiple_of(base, half) + start + k, 1), :] = jnp.full(
                    (1, 128), owner, jnp.int32
                )
        return carry

    fetch.wait()
    lax.fori_loop(0, half // 8, gather, 0)


def owner_of(device, columns):
    device = jnp.concatenate([device] * (columns // 128), axis=1)
    return lax.shift_right_logical(device, 1), device & 1


def combine_kernel(where_am_i, keep, got, meta, joined):
    chip, core = where_am_i[0], where_am_i[1]
    half = keep.shape[0]
    owner_chip, owner_core = owner_of(meta[pl.ds(core * half, half), :], keep.shape[1])
    mine = owner_chip == chip
    other = (mine & (owner_core != core)) | (~mine & ((chip == 0) & (core == 1)))
    joined[...] = jnp.where(other, got[...], keep[...])


def halves_kernel(
    where_am_i, joined, before, after, low, high, keep, got, meta, message, pivot_half, top_half
):
    chip, core = where_am_i[0], where_am_i[1]
    half = joined.shape[0]
    owner_chip, owner_core = owner_of(meta[pl.ds(core * half, half), :], joined.shape[1])
    ahead = (owner_chip - chip) & 3
    opposite = jnp.concatenate([low[...], high[...]], axis=0)
    pivot_rows = jnp.where(
        ahead == 0,
        joined[...],
        jnp.where(ahead == 1, after[...], jnp.where(ahead == 3, before[...], opposite)),
    )
    pivot_half[...] = pivot_rows
    top_rows = jnp.where(
        chip == 1, before[...], jnp.where(chip == 3, after[...], opposite)
    )
    top_half[...] = jnp.where(chip == 0, got[...], top_rows)
    message[...] = jnp.where(
        (ahead == 0) & (owner_core != core),
        jnp.where(chip == 0, keep[...], top_rows),
        pivot_rows,
    )


def pair_kernel(own, before, after, three, two):
    size = own.shape[0]
    for k, block in enumerate((own, before, after)):
        three[k * size : (k + 1) * size, :] = block[...]
        if k < 2:
            two[k * size : (k + 1) * size, :] = block[...]


Z_ORDER = (0, -1, 1, -3, -4, -2, 3, 2)


def line_kernel(three, far_before, far_after, line, square):
    for start, block in ((0, three), (24, far_before), (48, far_after)):
        line[start : start + block.shape[0], :] = block[...]
    square[...] = line[:, : square.shape[1]]


def final_kernel(
    where_am_i, places, t_ref, wh_ref, wl_ref, pivot_half, top_half, send, got, meta, out, pivot
):
    chip, core = where_am_i[0], where_am_i[1]
    half = pivot_half.shape[0]
    width = 2 * half
    device = chip * 2 + core
    owner_chip, owner_core = owner_of(
        meta[pl.ds((1 - core) * half, half), :], got.shape[1]
    )
    here = (owner_chip == chip) & (owner_core == core)
    pivot[pl.ds(core * half, half), :] = pivot_half[...]
    pivot[pl.ds((1 - core) * half, half), :] = jnp.where(here, send[...], got[...])
    out[...] = t_ref[...]

    def place(i, carry):
        packed = places[1 + i]
        slot = packed & 255
        target = lax.shift_right_logical(packed, 8) & 1023
        down = jnp.where(device == 0, lax.shift_right_logical(packed, 20), 0)
        index = slot & (half - 1)
        in_half = lax.shift_right_logical(slot, 7) == core
        row = jnp.where(
            device == 0,
            t_ref[pl.ds(down, 1), :],
            jnp.where(in_half, top_half[pl.ds(index, 1), :], got[pl.ds(index, 1), :]),
        )
        out[pl.ds(target, 1), :] = row
        return carry

    lax.fori_loop(0, places[0], place, 0)

    @pl.when(device == 0)
    def _():
        out[0:width, :] = jnp.zeros((width, out.shape[1]), jnp.float32)

    weights = wh_ref[...], wl_ref[...]
    out[...] -= product(weights, split(pivot[...]))


def weights_kernel(where_am_i, line0, line1, line2, line3, wh_ref, wl_ref, stacked):
    width = stacked.shape[0]
    rows = stacked.shape[1] - width
    y, z = where_am_i[2], where_am_i[3]
    size = line0.shape[0] // 8
    for step, line in enumerate((line0, line1, line2, line3)):
        for k, offset in enumerate(Z_ORDER):
            column = ((y - step) & 3) * 8 + ((z + offset) & 7)
            stacked[pl.ds(pl.multiple_of(column * size, size), size), :] = line[
                k * size : (k + 1) * size, :
            ]
    square = stacked[:, rows:]
    row = lax.broadcasted_iota(jnp.int32, (width, width), 0)
    col = lax.broadcasted_iota(jnp.int32, (width, width), 1)
    apart = row ^ col
    inv = jnp.where(row == col, 1.0, 0.0)
    level = 0
    while (1 << level) < width:
        size = 1 << level
        link = (lax.shift_right_logical(apart, level) == 1) & ((col & size) != 0)
        off = jnp.where(link, square, 0.0)
        if level == 0:
            inv = inv - off
        else:
            parts = split(inv)
            inv = inv - product(split(product(parts, split(off))), parts)
        level += 1
    weights = product(split(inv), split(stacked[:, :rows])).T
    high, low = split(weights)
    wh_ref[...] = high
    wl_ref[...] = low

    @pl.when((where_am_i[0] == 0) & (where_am_i[1] == 0))
    def _():
        high, low = split(-inv.T)
        wh_ref[0:width, :] = high
        wl_ref[0:width, :] = low


def device_step(trailing, panel_factors, pivots):
    rows, columns = trailing.shape
    width = pivots.shape[0]
    half = width // 2
    chip, core = lax.axis_index("x"), lax.axis_index("core")
    here = jnp.stack([chip, core, lax.axis_index("y"), lax.axis_index("z")]).astype(jnp.int32)

    panel = panel_factors.T
    before, after = along(panel, "z", 1), along(panel, "z", -1)
    three, two = pl.pallas_call(
        pair_kernel,
        out_shape=(f32(3 * 8, rows), f32(2 * 8, rows)),
        in_specs=[VMEM] * 3,
        out_specs=(VMEM,) * 2,
        compiler_params=PARAMS,
    )(panel, before, after)
    far_before, far_after = along(three, "z", 3), along(two, "z", -3)
    panels, square = pl.pallas_call(
        line_kernel,
        out_shape=(f32(64, rows), f32(64, width)),
        in_specs=[VMEM] * 3,
        out_specs=(VMEM,) * 2,
        compiler_params=PARAMS,
    )(three, far_before, far_after)
    moved = lax.ppermute(square, "core", [(0, 1)])
    square = jnp.where(core == 1, moved, square)
    moved = lax.ppermute(square, "x", [(0, 1)])
    square = jnp.where(chip == 1, moved, square)
    moved = lax.ppermute(square, "x", [(0, 3), (1, 2)])
    square = jnp.where(chip >= 2, moved, square)
    line = jnp.concatenate([panels, square], axis=1)
    lines = [along(line, "y", step) for step in (1, 2, 3)]
    half_weights = jax.ShapeDtypeStruct((rows, width), jnp.bfloat16)
    high, low = pl.pallas_call(
        weights_kernel,
        out_shape=(half_weights, half_weights),
        in_specs=[SMEM] + [VMEM] * 4,
        out_specs=(VMEM, VMEM),
        scratch_shapes=[pltpu.VMEM((width, rows + width), jnp.float32)],
        compiler_params=PARAMS,
    )(here, line, *lines)

    plan = pl.pallas_call(
        plan_kernel,
        out_shape=(
            f32(half, columns),
            f32(half, columns),
            jax.ShapeDtypeStruct((width, 128), jnp.int32),
            jax.ShapeDtypeStruct((512,), jnp.int32),
        ),
        in_specs=[SMEM, SMEM, pl.BlockSpec(memory_space=pltpu.HBM)],
        out_specs=(VMEM, VMEM, VMEM, SMEM),
        scratch_shapes=[
            pltpu.SMEM((rows * 8,), jnp.int32),
            pltpu.SMEM((width,), jnp.int32),
            pltpu.VMEM((rows, columns), jnp.float32),
            pltpu.SemaphoreType.DMA,
        ],
        compiler_params=PARAMS,
    )
    keep, send, meta, places = plan(
        pivots, here, pltpu.with_memory_space_constraint(trailing, pltpu.HBM)
    )
    got = swapped(send, "core", 1)
    combine = pl.pallas_call(
        combine_kernel,
        out_shape=f32(half, columns),
        in_specs=[SMEM, VMEM, VMEM, VMEM],
        out_specs=VMEM,
        compiler_params=PARAMS,
    )
    joined = combine(here, keep, got, meta)
    near_before, near_after = along(joined, "x", 1), along(joined, "x", -1)
    far_low = along(near_before[: half // 2], "x", 1)
    far_high = along(near_after[half // 2 :], "x", -1)
    halves = pl.pallas_call(
        halves_kernel,
        out_shape=(f32(half, columns),) * 3,
        in_specs=[SMEM] + [VMEM] * 8,
        out_specs=(VMEM,) * 3,
        compiler_params=PARAMS,
    )
    message, pivot_half, top_half = halves(
        here, joined, near_before, near_after, far_low, far_high, keep, got, meta
    )
    last = swapped(message, "core", 1)
    return pl.pallas_call(
        final_kernel,
        out_shape=f32(rows, columns),
        in_specs=[SMEM, SMEM] + [VMEM] * 8,
        out_specs=VMEM,
        scratch_shapes=[pltpu.VMEM((width, columns), jnp.float32)],
        compiler_params=PARAMS,
    )(here, places, trailing, high, low, pivot_half, top_half, send, last, meta)


def solution(mesh):
    torus = Mesh(mesh.devices.reshape(4, 2, 4, 8), ("x", "core", "y", "z"))
    return jax.shard_map(
        device_step,
        mesh=torus,
        in_specs=(P(ROW, COL), P(ROW, COL), P()),
        out_specs=P(ROW, COL),
        check_vma=False,
    )
```

time: 62.1 us -> 70.7 us (1.14)
  waiting for transfers between devices: 12.8 us -> 20.2 us
  starting transfers between devices: 31 us -> 33.8 us
  Pallas kernels: 15.5 us -> 14.4 us
  local copies, waits for them, and re-layouts: 2.3 us -> 1.34 us
    ppermute x11 -> x16, starting transfers between devices: 19.8 us -> 33.8 us  [the longest x11 21.5 us: along(): lax.ppermute(value, axis, [(i, (i + step) % size) for i in range(size)])]
    all_to_all x1 -> x0, starting transfers between devices: 11.2 us -> none  [on_device(): lax.all_to_all(copies, COL, split_axis=0, concat_axis=0, tiled=True)]
    ppermute x11 -> x16, waiting for transfers between devices: 12.8 us -> 20.2 us  [the longest x11 20.2 us: along(): lax.ppermute(value, axis, [(i, (i + step) % size) for i in range(size)])]
    pallas_call x6 -> x7, Pallas kernels: 15.5 us -> 14.4 us  [the longest x1 5.6 us: device_step(): plan(pivots, here, pltpu.with_memory_space_constraint(trailing, pltpu.HBM))]
    broadcast_in_dim x1 -> x0, local copies, waits for them, and re-layouts: 0.93 us -> none  [on_device(): copies = jnp.broadcast_to(block, (lax.axis_size(COL), *block.shape))]
    slice x1 -> x2, local copies, waits for them, and re-layouts: 0.77 us -> 0.02 us  [the longest x1 0.01 us: device_step(): far_high = along(near_after[half // 2:], 'x', -1)]
    unnamed x6, local copies, waits for them, and re-layouts: 0.6 us -> 1.32 us
  transfers between devices with their start and end apart: 12 -> 16, of which waited for: 10 -> 6; matrix products, arithmetic and copies ran while one was open for 0% -> 0% of each run, Pallas kernels for 20% -> 16%
where the time goes in v3:
time: 70.7 us; the launch traced here: 70.1 us
  starting transfers between devices  33.8 us (48%)
  waiting for transfers between devices  20.2 us (29%)
  Pallas kernels  14.4 us (20%)
  local copies, waits for them, and re-layouts  1.34 us (2%)
    ppermute x11, starting transfers between devices, along(): lax.ppermute(value, axis, [(i, (i + step) % size) for i in range(size)])  21.5 us
    ppermute x11, waiting for transfers between devices, along(): lax.ppermute(value, axis, [(i, (i + step) % size) for i in range(size)])  20.2 us
    ppermute x2, starting transfers between devices, swapped(): lax.ppermute(value, axis, [(i, i ^ bit) for i in range(lax.axis_size(axis...  6.03 us
    pallas_call x1, Pallas kernels, device_step(): plan(pivots, here, pltpu.with_memory_space_constraint(trailing, pltpu.HBM))  5.6 us
    pallas_call x1, Pallas kernels, device_step(): pl.pallas_call(weights_kernel, out_shape=(half_weights, half_weights), in...  4.79 us
    ppermute x1, starting transfers between devices, device_step(): moved = lax.ppermute(square, 'x', [(0, 1)])  3.12 us
    pallas_call x1, Pallas kernels, device_step(): pl.pallas_call(final_kernel, out_shape=f32(rows, columns), in_specs=[SMEM...  2.7 us
    ppermute x1, starting transfers between devices, device_step(): moved = lax.ppermute(square, 'x', [(0, 3), (1, 2)])  1.91 us
  transfers between devices with their start and end apart: 16, of which 6 were waited for; matrix products, arithmetic and copies ran while one was open for 0% of the time, Pallas kernels for 16%

profile of v3, /device:TPU:1, one launch (start us, length us, event | category | flops | bytes accessed | tf_op | source)
XLA Modules:
  0.0 70.1 jit_solution(10125228987568104780)
XLA Ops:
  0.0 2.5 %collective-permute-start = (f32[8,512]{1,0:T(8,128)}, f32[8,512]{1,0:T(8,128)S(1)}, u32[]{:S(2)}, u32[]{:S(2)}) collective-permute-start(f32[8,512]{1,0:T(8,128)} %bitcast.5), channel_id=1, source_target_pairs={{0,1},{1,2},{2,3},{3,4},{4,5},{5,6},{6,7},{7,0},{8,9},{9,10},{10,1... | collective-permute-start | bytes 49160 | tf_op jit(solution)/shard_map/ppermute | solution.py:23
  2.5 3.9 %collective-permute-start.1 = (f32[8,512]{1,0:T(8,128)}, f32[8,512]{1,0:T(8,128)S(1)}, u32[]{:S(2)}, u32[]{:S(2)}) collective-permute-start(f32[8,512]{1,0:T(8,128)} %bitcast.6), channel_id=1, source_target_pairs={{0,7},{1,0},{2,1},{3,2},{4,3},{5,4},{6,5},{7,6},{8,15},{9,8},{10,9... | collective-permute-start | bytes 49160 | tf_op jit(solution)/shard_map/ppermute | solution.py:23
  6.4 1.3 %collective-permute-done.before = f32[8,512]{1,0:T(8,128)S(1)} collective-permute-done((f32[8,512]{1,0:T(8,128)}, f32[8,512]{1,0:T(8,128)S(1)}, u32[]{:S(2)}, u32[]{:S(2)}) %collective-permute-start) | collective-permute-done | bytes 16416 | tf_op jit(solution)/shard_map/ppermute | solution.py:23
  7.7 0.7 %copy-done.1 = f32[512,8]{0,1:T(8,128)S(1)} copy-done((f32[512,8]{0,1:T(8,128)S(1)}, f32[512,8]{0,1:T(8,128)}, u32[]{:S(2)}) %copy-start.1) | copy-done | bytes 16408
  8.5 4.3 %collective-permute-start.2 = (f32[24,512]{1,0:T(8,128)S(1)}, f32[24,512]{1,0:T(8,128)S(1)}, u32[]{:S(2)}, u32[]{:S(2)}) collective-permute-start(f32[24,512]{1,0:T(8,128)S(1)} %get-tuple-element.19.three), channel_id=1, source_target_pairs={{0,3},{1,4},{2,5},{3,6},{4,7},{5,0},{6,1},{7,2},{8,11},{9,12},{10,... | collective-permute-start | bytes 147464 | tf_op jit(solution)/shard_map/ppermute | solution.py:23
  12.9 4.4 %collective-permute-done.3.far_after = f32[16,512]{1,0:T(8,128)S(1)} collective-permute-done((f32[16,512]{1,0:T(8,128)S(1)}, f32[16,512]{1,0:T(8,128)S(1)}, u32[]{:S(2)}, u32[]{:S(2)}) %collective-permute-start.3) | collective-permute-done | bytes 32800 | tf_op jit(solution)/shard_map/ppermute | solution.py:23
  17.3 1.3 %collective-permute-start.4 = (f32[64,256]{1,0:T(8,128)S(1)}, f32[64,256]{1,0:T(8,128)S(1)}, u32[]{:S(2)}, u32[]{:S(2)}) collective-permute-start(f32[64,256]{1,0:T(8,128)S(1)} %get-tuple-element.22), channel_id=1, source_target_pairs={{0,32},{1,33},{2,34},{3,35},{4,36},{5,37},{6,38},{7,39},{8,40},{9,... | collective-permute-start | bytes 196616 | tf_op jit(solution)/shard_map/ppermute | solution.py:256
  19.3 5.6 %shard_map.37 = (f32[128,512]{1,0:T(8,128)S(1)}, f32[128,512]{1,0:T(8,128)S(1)}, s32[256,128]{1,0:T(8,128)S(1)}, s32[512]{0:T(512)S(1)}) custom-call(s32[256]{0:T(256)S(1)} %copy-done.2, s32[4]{0:T(128)S(1)} %pad_add_fusion.where_am_i, f32[512,512]{1,0:T(8,128)} %t_ref.1), custom_call_target="tpu_custom_call" | custom-call | tf_op jit(solution)/shard_map/pallas_call | solution.py:292
  24.9 3.6 %collective-permute-start.10 = (f32[128,512]{1,0:T(8,128)S(1)}, f32[128,512]{1,0:T(8,128)S(1)}, u32[]{:S(2)}, u32[]{:S(2)}) collective-permute-start(f32[128,512]{1,0:T(8,128)S(1)} %get-tuple-element.26.send), channel_id=1, source_target_pairs={{0,32},{32,0},{1,33},{33,1},{2,34},{34,2},{3,35},{35,3},{4,36},{36... | collective-permute-start | bytes 786440 | tf_op jit(solution)/shard_map/ppermute | solution.py:27
  28.6 3.1 %collective-permute-start.5 = (f32[64,256]{1,0:T(8,128)S(1)}, f32[64,256]{1,0:T(8,128)S(1)}, u32[]{:S(2)}, u32[]{:S(2)}) collective-permute-start(f32[64,256]{1,0:T(8,128)S(1)} %broadcast_select_fusion), channel_id=1, source_target_pairs={{0,64},{1,65},{2,66},{3,67},{4,68},{5,69},{6,70},{7,71},{8,72},{9,... | collective-permute-start | bytes 196616 | tf_op jit(solution)/shard_map/ppermute | solution.py:258
  32.4 2.7 %collective-permute-start.12 = (f32[128,512]{1,0:T(8,128)S(1)}, f32[128,512]{1,0:T(8,128)S(1)}, u32[]{:S(2)}, u32[]{:S(2)}) collective-permute-start(f32[128,512]{1,0:T(8,128)S(1)} %shard_map.41.joined), channel_id=1, source_target_pairs={{0,192},{64,0},{128,64},{192,128},{1,193},{65,1},{129,65},{193,129... | collective-permute-start | bytes 786440 | tf_op jit(solution)/shard_map/ppermute | solution.py:23
  35.1 1.9 %collective-permute-start.6 = (f32[64,256]{1,0:T(8,128)S(1)}, f32[64,256]{1,0:T(8,128)S(1)}, u32[]{:S(2)}, u32[]{:S(2)}) collective-permute-start(f32[64,256]{1,0:T(8,128)S(1)} %broadcast_select_fusion.1), channel_id=1, source_target_pairs={{0,192},{64,128},{1,193},{65,129},{2,194},{66,130},{3,195},{67,131... | collective-permute-start | bytes 196616 | tf_op jit(solution)/shard_map/ppermute | solution.py:260
  37.0 4.1 %collective-permute-done.11.before = f32[128,512]{1,0:T(8,128)S(1)} collective-permute-done((f32[128,512]{1,0:T(8,128)S(1)}, f32[128,512]{1,0:T(8,128)S(1)}, u32[]{:S(2)}, u32[]{:S(2)}) %collective-permute-start.11) | collective-permute-done | bytes 262176 | tf_op jit(solution)/shard_map/ppermute | solution.py:23
  41.3 2.7 %collective-permute-start.14 = (f32[64,512]{1,0:T(8,128)S(1)}, f32[64,512]{1,0:T(8,128)S(1)}, u32[]{:S(2)}, u32[]{:S(2)}) collective-permute-start(f32[64,512]{1,0:T(8,128)S(1)} %slice.9), channel_id=1, source_target_pairs={{0,192},{64,0},{128,64},{192,128},{1,193},{65,1},{129,65},{193,129... | collective-permute-start | bytes 393224 | tf_op jit(solution)/shard_map/ppermute | solution.py:23
  44.0 2.2 %collective-permute-done.13.low = f32[64,512]{1,0:T(8,128)S(1)} collective-permute-done((f32[64,512]{1,0:T(8,128)S(1)}, f32[64,512]{1,0:T(8,128)S(1)}, u32[]{:S(2)}, u32[]{:S(2)}) %collective-permute-start.13) | collective-permute-done | bytes 131104 | tf_op jit(solution)/shard_map/ppermute | solution.py:23
  46.3 0.7 %shard_map.42 = (f32[128,512]{1,0:T(8,128)S(1)}, f32[128,512]{1,0:T(8,128)S(1)}, f32[128,512]{1,0:T(8,128)S(1)}) custom-call(s32[4]{0:T(128)S(1)} %pad_add_fusion.where_am_i, f32[128,512]{1,0:T(8,128)S(1)} %shard_map.41.joined, f32[128,512]{1,0:T(8,128)S(1)} %collective-permute-done.11.before, f32[128,512]{1,0:T(8,128)S(1)} %collective-permute-done.12.after, ...), custom_call_target="tpu_custom_call" | custom-call | tf_op jit(solution)/shard_map/pallas_call | solution.py:314
  47.0 2.4 %collective-permute-start.15 = (f32[128,512]{1,0:T(8,128)S(1)}, f32[128,512]{1,0:T(8,128)S(1)}, u32[]{:S(2)}, u32[]{:S(2)}) collective-permute-start(f32[128,512]{1,0:T(8,128)S(1)} %get-tuple-element.30), channel_id=1, source_target_pairs={{0,32},{32,0},{1,33},{33,1},{2,34},{34,2},{3,35},{35,3},{4,36},{36... | collective-permute-start | bytes 786440 | tf_op jit(solution)/shard_map/ppermute | solution.py:27
  49.4 1.4 %collective-permute-start.7 = (f32[64,768]{1,0:T(8,128)S(1)}, f32[64,768]{1,0:T(8,128)S(1)}, u32[]{:S(2)}, u32[]{:S(2)}) collective-permute-start(f32[64,768]{1,0:T(8,128)S(1)} %pad_maximum_fusion.line0), channel_id=1, source_target_pairs={{0,8},{8,16},{16,24},{24,0},{1,9},{9,17},{17,25},{25,1},{2,10},{10... | collective-permute-start | bytes 589832 | tf_op jit(solution)/shard_map/ppermute | solution.py:23
  50.8 2.6 %collective-permute-start.8 = (f32[64,768]{1,0:T(8,128)S(1)}, f32[64,768]{1,0:T(8,128)S(1)}, u32[]{:S(2)}, u32[]{:S(2)}) collective-permute-start(f32[64,768]{1,0:T(8,128)S(1)} %pad_maximum_fusion.line0), channel_id=1, source_target_pairs={{0,16},{8,24},{16,0},{24,8},{1,17},{9,25},{17,1},{25,9},{2,18},{10... | collective-permute-start | bytes 589832 | tf_op jit(solution)/shard_map/ppermute | solution.py:23
  53.4 1.1 %collective-permute-start.9 = (f32[64,768]{1,0:T(8,128)S(1)}, f32[64,768]{1,0:T(8,128)S(1)}, u32[]{:S(2)}, u32[]{:S(2)}) collective-permute-start(f32[64,768]{1,0:T(8,128)S(1)} %pad_maximum_fusion.line0), channel_id=1, source_target_pairs={{0,24},{8,0},{16,8},{24,16},{1,25},{9,1},{17,9},{25,17},{2,26},{10... | collective-permute-start | bytes 589832 | tf_op jit(solution)/shard_map/ppermute | solution.py:23
  54.5 2.8 %collective-permute-done.7.line1 = f32[64,768]{1,0:T(8,128)S(1)} collective-permute-done((f32[64,768]{1,0:T(8,128)S(1)}, f32[64,768]{1,0:T(8,128)S(1)}, u32[]{:S(2)}, u32[]{:S(2)}) %collective-permute-start.7) | collective-permute-done | bytes 196640 | tf_op jit(solution)/shard_map/ppermute | solution.py:23
  57.3 5.3 %collective-permute-done.8.line2 = f32[64,768]{1,0:T(8,128)S(1)} collective-permute-done((f32[64,768]{1,0:T(8,128)S(1)}, f32[64,768]{1,0:T(8,128)S(1)}, u32[]{:S(2)}, u32[]{:S(2)}) %collective-permute-start.8) | collective-permute-done | bytes 196640 | tf_op jit(solution)/shard_map/ppermute | solution.py:23
  62.6 4.8 %shard_map.40 = (bf16[512,256]{1,0:T(8,128)(2,1)S(1)}, bf16[512,256]{1,0:T(8,128)(2,1)S(1)}) custom-call(s32[4]{0:T(128)S(1)} %pad_add_fusion.where_am_i, f32[64,768]{1,0:T(8,128)S(1)} %pad_maximum_fusion.line0, f32[64,768]{1,0:T(8,128)S(1)} %collective-permute-done.7.line1, f32[64,768]{1,0:T(8,128)S(1)} %collective-permute-done.8.line2, ...), custom_call_target="tpu_custom_call" | custom-call | tf_op jit(solution)/shard_map/pallas_call | solution.py:265
  67.4 2.7 %shard_map.43 = f32[512,512]{1,0:T(8,128)} custom-call(s32[4]{0:T(128)S(1)} %pad_add_fusion.where_am_i, s32[512]{0:T(512)S(1)} %get-tuple-element.18.places, f32[512,512]{1,0:T(8,128)S(1)} %copy-done, bf16[512,256]{1,0:T(8,128)(2,1)S(1)} %get-tuple-element.23.wh_ref, bf16[512,256]{1,0:T(8,128)(2,1)S(1)} %get-tuple-element.24.wl_ref, ...), custom_call_target="tpu_custom_call" | custom-call | tf_op jit(solution)/shard_map/pallas_call | solution.py:318
  (28 shorter events, 1.7 us)
Async XLA Ops:
  0.0 7.7 %collective-permute-start = (f32[8,512]{1,0:T(8,128)}, f32[8,512]{1,0:T(8,128)S(1)}, u32[]{:S(2)}, u32[]{:S(2)}) collective-permute-start(f32[8,512]{1,0:T(8,128)} %bitcast.5), channel_id=1, source_target_pairs={{0,1},{1,2},{2,3},{3,4},{4,5},{5,6},{6,7},{7,0},{8,9},{9,10},{10,1... | collective-permute-start | bytes 49160 | tf_op jit(solution)/shard_map/ppermute | solution.py:23
  2.5 5.3 %collective-permute-start.1 = (f32[8,512]{1,0:T(8,128)}, f32[8,512]{1,0:T(8,128)S(1)}, u32[]{:S(2)}, u32[]{:S(2)}) collective-permute-start(f32[8,512]{1,0:T(8,128)} %bitcast.6), channel_id=1, source_target_pairs={{0,7},{1,0},{2,1},{3,2},{4,3},{5,4},{6,5},{7,6},{8,15},{9,8},{10,9... | collective-permute-start | bytes 49160 | tf_op jit(solution)/shard_map/ppermute | solution.py:23
  7.7 0.7 %copy-start.1 = (f32[512,8]{0,1:T(8,128)S(1)}, f32[512,8]{0,1:T(8,128)}, u32[]{:S(2)}) copy-start(f32[512,8]{0,1:T(8,128)} %param.4) | copy-start | bytes 49156
  8.5 8.9 %collective-permute-start.2 = (f32[24,512]{1,0:T(8,128)S(1)}, f32[24,512]{1,0:T(8,128)S(1)}, u32[]{:S(2)}, u32[]{:S(2)}) collective-permute-start(f32[24,512]{1,0:T(8,128)S(1)} %get-tuple-element.19.three), channel_id=1, source_target_pairs={{0,3},{1,4},{2,5},{3,6},{4,7},{5,0},{6,1},{7,2},{8,11},{9,12},{10,... | collective-permute-start | bytes 147464 | tf_op jit(solution)/shard_map/ppermute | solution.py:23
  12.7 4.6 %collective-permute-start.3 = (f32[16,512]{1,0:T(8,128)S(1)}, f32[16,512]{1,0:T(8,128)S(1)}, u32[]{:S(2)}, u32[]{:S(2)}) collective-permute-start(f32[16,512]{1,0:T(8,128)S(1)} %get-tuple-element.20), channel_id=1, source_target_pairs={{0,5},{1,6},{2,7},{3,0},{4,1},{5,2},{6,3},{7,4},{8,13},{9,14},{10,... | collective-permute-start | bytes 98312 | tf_op jit(solution)/shard_map/ppermute | solution.py:23
  17.3 11.2 %collective-permute-start.4 = (f32[64,256]{1,0:T(8,128)S(1)}, f32[64,256]{1,0:T(8,128)S(1)}, u32[]{:S(2)}, u32[]{:S(2)}) collective-permute-start(f32[64,256]{1,0:T(8,128)S(1)} %get-tuple-element.22), channel_id=1, source_target_pairs={{0,32},{1,33},{2,34},{3,35},{4,36},{5,37},{6,38},{7,39},{8,40},{9,... | collective-permute-start | bytes 196616 | tf_op jit(solution)/shard_map/ppermute | solution.py:256
  18.6 0.7 copy-start.2
  24.9 6.8 %collective-permute-start.10 = (f32[128,512]{1,0:T(8,128)S(1)}, f32[128,512]{1,0:T(8,128)S(1)}, u32[]{:S(2)}, u32[]{:S(2)}) collective-permute-start(f32[128,512]{1,0:T(8,128)S(1)} %get-tuple-element.26.send), channel_id=1, source_target_pairs={{0,32},{32,0},{1,33},{33,1},{2,34},{34,2},{3,35},{35,3},{4,36},{36... | collective-permute-start | bytes 786440 | tf_op jit(solution)/shard_map/ppermute | solution.py:27
  28.6 6.5 %collective-permute-start.5 = (f32[64,256]{1,0:T(8,128)S(1)}, f32[64,256]{1,0:T(8,128)S(1)}, u32[]{:S(2)}, u32[]{:S(2)}) collective-permute-start(f32[64,256]{1,0:T(8,128)S(1)} %broadcast_select_fusion), channel_id=1, source_target_pairs={{0,64},{1,65},{2,66},{3,67},{4,68},{5,69},{6,70},{7,71},{8,72},{9,... | collective-permute-start | bytes 196616 | tf_op jit(solution)/shard_map/ppermute | solution.py:258
  32.3 8.8 %collective-permute-start.11 = (f32[128,512]{1,0:T(8,128)S(1)}, f32[128,512]{1,0:T(8,128)S(1)}, u32[]{:S(2)}, u32[]{:S(2)}) collective-permute-start(f32[128,512]{1,0:T(8,128)S(1)} %shard_map.41.joined), channel_id=1, source_target_pairs={{0,64},{64,128},{128,192},{192,0},{1,65},{65,129},{129,193},{193,1... | collective-permute-start | bytes 786440 | tf_op jit(solution)/shard_map/ppermute | solution.py:23
  32.4 8.9 %collective-permute-start.12 = (f32[128,512]{1,0:T(8,128)S(1)}, f32[128,512]{1,0:T(8,128)S(1)}, u32[]{:S(2)}, u32[]{:S(2)}) collective-permute-start(f32[128,512]{1,0:T(8,128)S(1)} %shard_map.41.joined), channel_id=1, source_target_pairs={{0,192},{64,0},{128,64},{192,128},{1,193},{65,1},{129,65},{193,129... | collective-permute-start | bytes 786440 | tf_op jit(solution)/shard_map/ppermute | solution.py:23
  35.1 8.9 %collective-permute-start.6 = (f32[64,256]{1,0:T(8,128)S(1)}, f32[64,256]{1,0:T(8,128)S(1)}, u32[]{:S(2)}, u32[]{:S(2)}) collective-permute-start(f32[64,256]{1,0:T(8,128)S(1)} %broadcast_select_fusion.1), channel_id=1, source_target_pairs={{0,192},{64,128},{1,193},{65,129},{2,194},{66,130},{3,195},{67,131... | collective-permute-start | bytes 196616 | tf_op jit(solution)/shard_map/ppermute | solution.py:260
  41.2 5.1 %collective-permute-start.13 = (f32[64,512]{1,0:T(8,128)S(1)}, f32[64,512]{1,0:T(8,128)S(1)}, u32[]{:S(2)}, u32[]{:S(2)}) collective-permute-start(f32[64,512]{1,0:T(8,128)S(1)} %slice.8), channel_id=1, source_target_pairs={{0,64},{64,128},{128,192},{192,0},{1,65},{65,129},{129,193},{193,1... | collective-permute-start | bytes 393224 | tf_op jit(solution)/shard_map/ppermute | solution.py:23
  41.3 5.0 %collective-permute-start.14 = (f32[64,512]{1,0:T(8,128)S(1)}, f32[64,512]{1,0:T(8,128)S(1)}, u32[]{:S(2)}, u32[]{:S(2)}) collective-permute-start(f32[64,512]{1,0:T(8,128)S(1)} %slice.9), channel_id=1, source_target_pairs={{0,192},{64,0},{128,64},{192,128},{1,193},{65,1},{129,65},{193,129... | collective-permute-start | bytes 393224 | tf_op jit(solution)/shard_map/ppermute | solution.py:23
  44.0 23.4 %copy-start = (f32[512,512]{1,0:T(8,128)S(1)}, f32[512,512]{1,0:T(8,128)}, u32[]{:S(2)}) copy-start(f32[512,512]{1,0:T(8,128)} %t_ref.1) | copy-start | bytes 3145732
  47.0 20.4 %collective-permute-start.15 = (f32[128,512]{1,0:T(8,128)S(1)}, f32[128,512]{1,0:T(8,128)S(1)}, u32[]{:S(2)}, u32[]{:S(2)}) collective-permute-start(f32[128,512]{1,0:T(8,128)S(1)} %get-tuple-element.30), channel_id=1, source_target_pairs={{0,32},{32,0},{1,33},{33,1},{2,34},{34,2},{3,35},{35,3},{4,36},{36... | collective-permute-start | bytes 786440 | tf_op jit(solution)/shard_map/ppermute | solution.py:27
  49.4 7.9 %collective-permute-start.7 = (f32[64,768]{1,0:T(8,128)S(1)}, f32[64,768]{1,0:T(8,128)S(1)}, u32[]{:S(2)}, u32[]{:S(2)}) collective-permute-start(f32[64,768]{1,0:T(8,128)S(1)} %pad_maximum_fusion.line0), channel_id=1, source_target_pairs={{0,8},{8,16},{16,24},{24,0},{1,9},{9,17},{17,25},{25,1},{2,10},{10... | collective-permute-start | bytes 589832 | tf_op jit(solution)/shard_map/ppermute | solution.py:23
  50.8 11.8 %collective-permute-start.8 = (f32[64,768]{1,0:T(8,128)S(1)}, f32[64,768]{1,0:T(8,128)S(1)}, u32[]{:S(2)}, u32[]{:S(2)}) collective-permute-start(f32[64,768]{1,0:T(8,128)S(1)} %pad_maximum_fusion.line0), channel_id=1, source_target_pairs={{0,16},{8,24},{16,0},{24,8},{1,17},{9,25},{17,1},{25,9},{2,18},{10... | collective-permute-start | bytes 589832 | tf_op jit(solution)/shard_map/ppermute | solution.py:23
  53.4 9.2 %collective-permute-start.9 = (f32[64,768]{1,0:T(8,128)S(1)}, f32[64,768]{1,0:T(8,128)S(1)}, u32[]{:S(2)}, u32[]{:S(2)}) collective-permute-start(f32[64,768]{1,0:T(8,128)S(1)} %pad_maximum_fusion.line0), channel_id=1, source_target_pairs={{0,24},{8,0},{16,8},{24,16},{1,25},{9,1},{17,9},{25,17},{2,26},{10... | collective-permute-start | bytes 589832 | tf_op jit(solution)/shard_map/ppermute | solution.py:23

commit v4 on v3

--- a/solution.py
+++ b/solution.py
@@ -33,13 +33,14 @@
 
 
 def product(left, right):
-    def dot(a, b):
-        return jnp.dot(a, b, preferred_element_type=jnp.float32)
-
-    return dot(left[0], right[0]) + (dot(left[0], right[1]) + dot(left[1], right[0]))
-
-
-def plan_kernel(piv, where_am_i, t_hbm, keep, send, meta, places, order, picks, t_ref, arrived):
+    return jnp.dot(
+        jnp.concatenate([left[0], left[0], left[1]], axis=1),
+        jnp.concatenate([right[0], right[1], right[0]], axis=0),
+        preferred_element_type=jnp.float32,
+    )
+
+
+def plan_kernel(piv, where_am_i, t_hbm, keep, send, meta, order, picks, t_ref, arrived):
     fetch = pltpu.make_async_copy(t_hbm, t_ref, arrived)
     fetch.start()
     width = piv.shape[0]
@@ -67,16 +68,13 @@
 
     lax.fori_loop(0, width, swap, 0, unroll=16)
 
-    def pick(slot, count):
+    def pick(slot, carry):
         src = order[slot]
-        down = order[src]
-        local = src & (rows - 1)
         own = lax.shift_right_logical(src, shift) == device
-        picks[slot] = jnp.where(own, local, down & (rows - 1))
-        places[1 + count] = slot | (local << 8) | (down << 20)
-        return count + jnp.where(own & (src >= width), 1, 0)
-
-    places[0] = lax.fori_loop(0, width, pick, 0, unroll=8)
+        picks[slot] = jnp.where(own, src, order[src]) & (rows - 1)
+        return carry
+
+    lax.fori_loop(0, width, pick, 0, unroll=16)
 
     def gather(group, carry):
         for base, out in ((core * half, keep), ((1 - core) * half, send)):
@@ -92,6 +90,21 @@
 
     fetch.wait()
     lax.fori_loop(0, half // 8, gather, 0)
+
+
+def list_kernel(order, where_am_i, places):
+    width = places.shape[0] // 2
+    device = where_am_i[0] * 2 + where_am_i[1]
+    rows = order.shape[0] // 8
+    shift = rows.bit_length() - 1
+
+    def visit(slot, count):
+        src = order[slot]
+        places[1 + count] = slot | ((src & (rows - 1)) << 8) | (order[src] << 20)
+        own = lax.shift_right_logical(src, shift) == device
+        return count + jnp.where(own & (src >= width), 1, 0)
+
+    places[0] = lax.fori_loop(0, width, visit, 0, unroll=8)
 
 
 def owner_of(device, columns):
@@ -151,9 +164,10 @@
 
 
 def final_kernel(
-    where_am_i, places, t_ref, wh_ref, wl_ref, pivot_half, top_half, send, got, meta, out, pivot
+    where_am_i, places, t_ref, w_ref, pivot_half, top_half, send, got, meta, result, pivot, out, done
 ):
     chip, core = where_am_i[0], where_am_i[1]
+    rows = t_ref.shape[0]
     half = pivot_half.shape[0]
     width = 2 * half
     device = chip * 2 + core
@@ -186,11 +200,21 @@
     def _():
         out[0:width, :] = jnp.zeros((width, out.shape[1]), jnp.float32)
 
-    weights = wh_ref[...], wl_ref[...]
-    out[...] -= product(weights, split(pivot[...]))
-
-
-def weights_kernel(where_am_i, line0, line1, line2, line3, wh_ref, wl_ref, stacked):
+    high, low = split(pivot[...])
+    rows_in = jnp.concatenate([high, low, high], axis=0)
+    copies = []
+    for k in range(4):
+        band = pl.ds(k * rows // 4, rows // 4)
+        out[band, :] -= jnp.dot(
+            w_ref[band, :], rows_in, preferred_element_type=jnp.float32
+        )
+        copies.append(pltpu.make_async_copy(out.at[band, :], result.at[band, :], done.at[k]))
+        copies[-1].start()
+    for copy in copies:
+        copy.wait()
+
+
+def weights_kernel(where_am_i, line0, line1, line2, line3, w_ref, stacked):
     width = stacked.shape[0]
     rows = stacked.shape[1] - width
     y, z = where_am_i[2], where_am_i[3]
@@ -201,32 +225,61 @@
             stacked[pl.ds(pl.multiple_of(column * size, size), size), :] = line[
                 k * size : (k + 1) * size, :
             ]
-    square = stacked[:, rows:]
-    row = lax.broadcasted_iota(jnp.int32, (width, width), 0)
-    col = lax.broadcasted_iota(jnp.int32, (width, width), 1)
+    block = width // 2
+    row = lax.broadcasted_iota(jnp.int32, (block, block), 0)
+    col = lax.broadcasted_iota(jnp.int32, (block, block), 1)
     apart = row ^ col
-    inv = jnp.where(row == col, 1.0, 0.0)
-    level = 0
-    while (1 << level) < width:
-        size = 1 << level
-        link = (lax.shift_right_logical(apart, level) == 1) & ((col & size) != 0)
-        off = jnp.where(link, square, 0.0)
-        if level == 0:
-            inv = inv - off
-        else:
-            parts = split(inv)
-            inv = inv - product(split(product(parts, split(off))), parts)
-        level += 1
-    weights = product(split(inv), split(stacked[:, :rows])).T
+
+    def inverse(square):
+        inv = jnp.where(row == col, 1.0, 0.0)
+        level = 0
+        while (1 << level) < block:
+            wide = (1 << level + 1) < block
+            far = lax.shift_right_logical(apart, level)
+            link = (far > 0) & (far < (4 if wide else 2)) & (row < col)
+            off = split(jnp.where(link, square, 0.0))
+            if level == 0:
+                step = jnp.where(link, square, 0.0)
+                parts = split(step)
+                inv = inv - step
+            else:
+                parts = split(product(split(inv), off))
+                inv = inv - product(parts, split(inv))
+            if wide:
+                twice = product(parts, parts)
+                inv = inv + product(split(twice), split(inv))
+            level += 2
+        return inv
+
+    first = inverse(stacked[0:block, rows : rows + block])
+    second = inverse(stacked[block:, rows + block :])
+    corner = product(
+        split(product(split(first), split(stacked[0:block, rows + block :]))), split(second)
+    )
+    inv = jnp.concatenate(
+        [
+            jnp.concatenate([first, -corner], axis=1),
+            jnp.concatenate([jnp.zeros_like(corner), second], axis=1),
+        ],
+        axis=0,
+    )
+    factors = stacked[:, :rows].T
+    top = (where_am_i[0] == 0) & (where_am_i[1] == 0)
+    here = lax.broadcasted_iota(jnp.int32, (width, width), 0)
+    there = lax.broadcasted_iota(jnp.int32, (width, width), 1)
+    minus_one = jnp.where(here == there, -1.0, 0.0)
+    factors = jnp.concatenate(
+        [jnp.where(top, minus_one, factors[0:width, :]), factors[width:, :]], axis=0
+    )
+    a, b = split(factors), split(inv)
+    weights = lax.dot_general(
+        jnp.concatenate([a[0], a[0], a[1]], axis=1),
+        jnp.concatenate([b[0], b[1], b[0]], axis=1),
+        (((1,), (1,)), ((), ())),
+        preferred_element_type=jnp.float32,
+    )
     high, low = split(weights)
-    wh_ref[...] = high
-    wl_ref[...] = low
-
-    @pl.when((where_am_i[0] == 0) & (where_am_i[1] == 0))
-    def _():
-        high, low = split(-inv.T)
-        wh_ref[0:width, :] = high
-        wl_ref[0:width, :] = low
+    w_ref[...] = jnp.concatenate([high, high, low], axis=1)
 
 
 def device_step(trailing, panel_factors, pivots):
@@ -253,20 +306,21 @@
         out_specs=(VMEM,) * 2,
         compiler_params=PARAMS,
     )(three, far_before, far_after)
-    moved = lax.ppermute(square, "core", [(0, 1)])
+    moved = swapped(square, "core", 1)
     square = jnp.where(core == 1, moved, square)
-    moved = lax.ppermute(square, "x", [(0, 1)])
-    square = jnp.where(chip == 1, moved, square)
-    moved = lax.ppermute(square, "x", [(0, 3), (1, 2)])
-    square = jnp.where(chip >= 2, moved, square)
+    ways = [(i, (i + (2 if i % 2 == 0 else 6)) % 8) for i in range(8)]
+    near = lax.ppermute(square, ROW, ways)
+    far = along(square, "x", 2)
+    square = jnp.where(chip == 0, square, jnp.where(chip == 2, far, near))
+    moved = swapped(square, "core", 1)
+    square = jnp.where((chip & 1 == 1) & (core == (chip >> 1 ^ 1)), moved, square)
     line = jnp.concatenate([panels, square], axis=1)
     lines = [along(line, "y", step) for step in (1, 2, 3)]
-    half_weights = jax.ShapeDtypeStruct((rows, width), jnp.bfloat16)
-    high, low = pl.pallas_call(
+    weights = pl.pallas_call(
         weights_kernel,
-        out_shape=(half_weights, half_weights),
+        out_shape=jax.ShapeDtypeStruct((rows, 3 * width), jnp.bfloat16),
         in_specs=[SMEM] + [VMEM] * 4,
-        out_specs=(VMEM, VMEM),
+        out_specs=VMEM,
         scratch_shapes=[pltpu.VMEM((width, rows + width), jnp.float32)],
         compiler_params=PARAMS,
     )(here, line, *lines)
@@ -277,19 +331,18 @@
             f32(half, columns),
             f32(half, columns),
             jax.ShapeDtypeStruct((width, 128), jnp.int32),
-            jax.ShapeDtypeStruct((512,), jnp.int32),
+            jax.ShapeDtypeStruct((rows * 8,), jnp.int32),
         ),
         in_specs=[SMEM, SMEM, pl.BlockSpec(memory_space=pltpu.HBM)],
         out_specs=(VMEM, VMEM, VMEM, SMEM),
         scratch_shapes=[
-            pltpu.SMEM((rows * 8,), jnp.int32),
             pltpu.SMEM((width,), jnp.int32),
             pltpu.VMEM((rows, columns), jnp.float32),
             pltpu.SemaphoreType.DMA,
         ],
         compiler_params=PARAMS,
     )
-    keep, send, meta, places = plan(
+    keep, send, meta, order = plan(
         pivots, here, pltpu.with_memory_space_constraint(trailing, pltpu.HBM)
     )
     got = swapped(send, "core", 1)
@@ -314,15 +367,27 @@
     message, pivot_half, top_half = halves(
         here, joined, near_before, near_after, far_low, far_high, keep, got, meta
     )
+    listing = pl.pallas_call(
+        list_kernel,
+        out_shape=jax.ShapeDtypeStruct((2 * width,), jnp.int32),
+        in_specs=[SMEM, SMEM],
+        out_specs=SMEM,
+        compiler_params=PARAMS,
+    )
+    places = listing(order, here)
     last = swapped(message, "core", 1)
     return pl.pallas_call(
         final_kernel,
         out_shape=f32(rows, columns),
-        in_specs=[SMEM, SMEM] + [VMEM] * 8,
-        out_specs=VMEM,
-        scratch_shapes=[pltpu.VMEM((width, columns), jnp.float32)],
-        compiler_params=PARAMS,
-    )(here, places, trailing, high, low, pivot_half, top_half, send, last, meta)
+        in_specs=[SMEM, SMEM] + [VMEM] * 7,
+        out_specs=pl.BlockSpec(memory_space=pltpu.HBM),
+        scratch_shapes=[
+            pltpu.VMEM((width, columns), jnp.float32),
+            pltpu.VMEM((rows, columns), jnp.float32),
+            pltpu.SemaphoreType.DMA((4,)),
+        ],
+        compiler_params=PARAMS,
+    )(here, places, trailing, weights, pivot_half, top_half, send, last, meta)
 
 
 def solution(mesh):

time: 70.7 us -> 69.8 us (0.987)
  Pallas kernels: 14.4 us -> 15.3 us
  waiting for transfers between devices: 20.2 us -> 19.3 us
  starting transfers between devices: 33.8 us -> 33 us
    ppermute x3 -> x1, starting transfers between devices: 6.32 us -> 0.86 us  [device_step(): near = lax.ppermute(square, ROW, ways)]
    ppermute x2 -> x4, starting transfers between devices: 6.03 us -> 8.41 us  [swapped(): lax.ppermute(value, axis, [(i, i ^ bit) for i in range(lax.axis_size(axis...]
    ppermute x11 -> x12, starting transfers between devices: 21.5 us -> 23.7 us  [along(): lax.ppermute(value, axis, [(i, (i + step) % size) for i in range(size)])]
    pallas_call x1 -> x2, Pallas kernels: 4.79 us -> 6.64 us  [the longest x1 3.88 us: device_step(): pl.pallas_call(weights_kernel, out_shape=jax.ShapeDtypeStruct((rows, 3 *...]
    ppermute x11 -> x12, waiting for transfers between devices: 20.2 us -> 19.3 us  [along(): lax.ppermute(value, axis, [(i, (i + step) % size) for i in range(size)])]
    pallas_call x1, Pallas kernels: 5.6 us -> 4.84 us  [device_step(): plan(pivots, here, pltpu.with_memory_space_constraint(trailing, pltpu.HBM))]
  transfers between devices with their start and end apart: 16 -> 17, of which waited for: 6 -> 6; matrix products, arithmetic and copies ran while one was open for 0% -> 0% of each run, Pallas kernels for 16% -> 17%
where the time goes in v4:
time: 69.8 us; the launch traced here: 69.4 us
  starting transfers between devices  33 us (47%)
  waiting for transfers between devices  19.3 us (28%)
  Pallas kernels  15.3 us (22%)
  local copies, waits for them, and re-layouts  1.35 us (2%)
    ppermute x12, starting transfers between devices, along(): lax.ppermute(value, axis, [(i, (i + step) % size) for i in range(size)])  23.7 us
    ppermute x12, waiting for transfers between devices, along(): lax.ppermute(value, axis, [(i, (i + step) % size) for i in range(size)])  19.3 us
    ppermute x4, starting transfers between devices, swapped(): lax.ppermute(value, axis, [(i, i ^ bit) for i in range(lax.axis_size(axis...  8.41 us
    pallas_call x1, Pallas kernels, device_step(): plan(pivots, here, pltpu.with_memory_space_constraint(trailing, pltpu.HBM))  4.84 us
    pallas_call x1, Pallas kernels, device_step(): pl.pallas_call(weights_kernel, out_shape=jax.ShapeDtypeStruct((rows, 3 *...  3.88 us
    pallas_call x1, Pallas kernels, device_step(): places = listing(order, here)  2.75 us
    pallas_call x1, Pallas kernels, device_step(): pl.pallas_call(final_kernel, out_shape=f32(rows, columns), in_specs=[SMEM...  2.51 us
  transfers between devices with their start and end apart: 17, of which 6 were waited for; matrix products, arithmetic and copies ran while one was open for 0% of the time, Pallas kernels for 17%

profile of v4, /device:TPU:1, one launch (start us, length us, event | category | flops | bytes accessed | tf_op | source)
XLA Modules:
  0.0 69.4 jit_solution(10357184275170273971)
XLA Ops:
  0.0 2.5 %collective-permute-start = (f32[8,512]{1,0:T(8,128)}, f32[8,512]{1,0:T(8,128)S(1)}, u32[]{:S(2)}, u32[]{:S(2)}) collective-permute-start(f32[8,512]{1,0:T(8,128)} %bitcast.5), channel_id=1, source_target_pairs={{0,1},{1,2},{2,3},{3,4},{4,5},{5,6},{6,7},{7,0},{8,9},{9,10},{10,1... | collective-permute-start | bytes 49160 | tf_op jit(solution)/shard_map/ppermute | solution.py:23
  2.5 3.9 %collective-permute-start.1 = (f32[8,512]{1,0:T(8,128)}, f32[8,512]{1,0:T(8,128)S(1)}, u32[]{:S(2)}, u32[]{:S(2)}) collective-permute-start(f32[8,512]{1,0:T(8,128)} %bitcast.6), channel_id=1, source_target_pairs={{0,7},{1,0},{2,1},{3,2},{4,3},{5,4},{6,5},{7,6},{8,15},{9,8},{10,9... | collective-permute-start | bytes 49160 | tf_op jit(solution)/shard_map/ppermute | solution.py:23
  6.4 1.3 %collective-permute-done.before = f32[8,512]{1,0:T(8,128)S(1)} collective-permute-done((f32[8,512]{1,0:T(8,128)}, f32[8,512]{1,0:T(8,128)S(1)}, u32[]{:S(2)}, u32[]{:S(2)}) %collective-permute-start) | collective-permute-done | bytes 16416 | tf_op jit(solution)/shard_map/ppermute | solution.py:23
  7.7 0.7 %copy-done.1 = f32[512,8]{0,1:T(8,128)S(1)} copy-done((f32[512,8]{0,1:T(8,128)S(1)}, f32[512,8]{0,1:T(8,128)}, u32[]{:S(2)}) %copy-start.1) | copy-done | bytes 16408
  8.5 4.3 %collective-permute-start.2 = (f32[24,512]{1,0:T(8,128)S(1)}, f32[24,512]{1,0:T(8,128)S(1)}, u32[]{:S(2)}, u32[]{:S(2)}) collective-permute-start(f32[24,512]{1,0:T(8,128)S(1)} %get-tuple-element.17.three), channel_id=1, source_target_pairs={{0,3},{1,4},{2,5},{3,6},{4,7},{5,0},{6,1},{7,2},{8,11},{9,12},{10,... | collective-permute-start | bytes 147464 | tf_op jit(solution)/shard_map/ppermute | solution.py:23
  12.9 4.4 %collective-permute-done.3.far_after = f32[16,512]{1,0:T(8,128)S(1)} collective-permute-done((f32[16,512]{1,0:T(8,128)S(1)}, f32[16,512]{1,0:T(8,128)S(1)}, u32[]{:S(2)}, u32[]{:S(2)}) %collective-permute-start.3) | collective-permute-done | bytes 32800 | tf_op jit(solution)/shard_map/ppermute | solution.py:23
  17.3 3.6 %collective-permute-start.4 = (f32[64,256]{1,0:T(8,128)S(1)}, f32[64,256]{1,0:T(8,128)S(1)}, u32[]{:S(2)}, u32[]{:S(2)}) collective-permute-start(f32[64,256]{1,0:T(8,128)S(1)} %get-tuple-element.20), channel_id=1, source_target_pairs={{0,32},{32,0},{1,33},{33,1},{2,34},{34,2},{3,35},{35,3},{4,36},{36... | collective-permute-start | bytes 196616 | tf_op jit(solution)/shard_map/ppermute | solution.py:27
  21.6 4.8 %shard_map.37 = (f32[128,512]{1,0:T(8,128)S(1)}, f32[128,512]{1,0:T(8,128)S(1)}, s32[256,128]{1,0:T(8,128)S(1)}, s32[4096]{0:T(1024)S(1)}) custom-call(s32[256]{0:T(256)S(1)} %copy-done.2, s32[4]{0:T(128)S(1)} %pad_add_fusion.where_am_i, f32[512,512]{1,0:T(8,128)} %t_ref.1), custom_call_target="tpu_custom_call" | custom-call | tf_op jit(solution)/shard_map/pallas_call | solution.py:345
  26.6 2.8 %collective-permute-start.5 = (f32[64,256]{1,0:T(8,128)S(1)}, f32[64,256]{1,0:T(8,128)S(1)}, u32[]{:S(2)}, u32[]{:S(2)}) collective-permute-start(f32[64,256]{1,0:T(8,128)S(1)} %broadcast_select_fusion), channel_id=1, source_target_pairs={{0,128},{64,192},{128,0},{192,64},{1,129},{65,193},{129,1},{193,65... | collective-permute-start | bytes 196616 | tf_op jit(solution)/shard_map/ppermute | solution.py:23
  29.4 0.9 %collective-permute-start.6 = (f32[64,256]{1,0:T(8,128)S(1)}, f32[64,256]{1,0:T(8,128)S(1)}, u32[]{:S(2)}, u32[]{:S(2)}) collective-permute-start(f32[64,256]{1,0:T(8,128)S(1)} %broadcast_select_fusion), channel_id=1, source_target_pairs={{0,64},{32,224},{64,128},{96,32},{128,192},{160,96},{192,0},{224,1... | collective-permute-start | bytes 196616 | tf_op jit(solution)/shard_map/ppermute | solution.py:312
  31.6 2.1 %collective-permute-start.13 = (f32[128,512]{1,0:T(8,128)S(1)}, f32[128,512]{1,0:T(8,128)S(1)}, u32[]{:S(2)}, u32[]{:S(2)}) collective-permute-start(f32[128,512]{1,0:T(8,128)S(1)} %shard_map.42.joined), channel_id=1, source_target_pairs={{0,192},{64,0},{128,64},{192,128},{1,193},{65,1},{129,65},{193,129... | collective-permute-start | bytes 786440 | tf_op jit(solution)/shard_map/ppermute | solution.py:23
  33.7 2.5 %collective-permute-start.7 = (f32[64,256]{1,0:T(8,128)S(1)}, f32[64,256]{1,0:T(8,128)S(1)}, u32[]{:S(2)}, u32[]{:S(2)}) collective-permute-start(f32[64,256]{1,0:T(8,128)S(1)} %select_select_fusion), channel_id=1, source_target_pairs={{0,32},{32,0},{1,33},{33,1},{2,34},{34,2},{3,35},{35,3},{4,36},{36... | collective-permute-start | bytes 196616 | tf_op jit(solution)/shard_map/ppermute | solution.py:27
  36.2 4.2 %collective-permute-done.12.before = f32[128,512]{1,0:T(8,128)S(1)} collective-permute-done((f32[128,512]{1,0:T(8,128)S(1)}, f32[128,512]{1,0:T(8,128)S(1)}, u32[]{:S(2)}, u32[]{:S(2)}) %collective-permute-start.12) | collective-permute-done | bytes 262176 | tf_op jit(solution)/shard_map/ppermute | solution.py:23
  40.5 2.7 %collective-permute-start.15 = (f32[64,512]{1,0:T(8,128)S(1)}, f32[64,512]{1,0:T(8,128)S(1)}, u32[]{:S(2)}, u32[]{:S(2)}) collective-permute-start(f32[64,512]{1,0:T(8,128)S(1)} %slice.9), channel_id=1, source_target_pairs={{0,192},{64,0},{128,64},{192,128},{1,193},{65,1},{129,65},{193,129... | collective-permute-start | bytes 393224 | tf_op jit(solution)/shard_map/ppermute | solution.py:23
  43.2 2.2 %collective-permute-done.14.low = f32[64,512]{1,0:T(8,128)S(1)} collective-permute-done((f32[64,512]{1,0:T(8,128)S(1)}, f32[64,512]{1,0:T(8,128)S(1)}, u32[]{:S(2)}, u32[]{:S(2)}) %collective-permute-start.14) | collective-permute-done | bytes 131104 | tf_op jit(solution)/shard_map/ppermute | solution.py:23
  45.5 0.7 %shard_map.43 = (f32[128,512]{1,0:T(8,128)S(1)}, f32[128,512]{1,0:T(8,128)S(1)}, f32[128,512]{1,0:T(8,128)S(1)}) custom-call(s32[4]{0:T(128)S(1)} %pad_add_fusion.where_am_i, f32[128,512]{1,0:T(8,128)S(1)} %shard_map.42.joined, f32[128,512]{1,0:T(8,128)S(1)} %collective-permute-done.12.before, f32[128,512]{1,0:T(8,128)S(1)} %collective-permute-done.13.after, ...), custom_call_target="tpu_custom_call" | custom-call | tf_op jit(solution)/shard_map/pallas_call | solution.py:367
  46.2 2.2 %collective-permute-start.16 = (f32[128,512]{1,0:T(8,128)S(1)}, f32[128,512]{1,0:T(8,128)S(1)}, u32[]{:S(2)}, u32[]{:S(2)}) collective-permute-start(f32[128,512]{1,0:T(8,128)S(1)} %get-tuple-element.26), channel_id=1, source_target_pairs={{0,32},{32,0},{1,33},{33,1},{2,34},{34,2},{3,35},{35,3},{4,36},{36... | collective-permute-start | bytes 786440 | tf_op jit(solution)/shard_map/ppermute | solution.py:27
  48.4 2.8 %collective-permute-start.10 = (f32[64,768]{1,0:T(8,128)S(1)}, f32[64,768]{1,0:T(8,128)S(1)}, u32[]{:S(2)}, u32[]{:S(2)}) collective-permute-start(f32[64,768]{1,0:T(8,128)S(1)} %pad_maximum_fusion.line0), channel_id=1, source_target_pairs={{0,24},{8,0},{16,8},{24,16},{1,25},{9,1},{17,9},{25,17},{2,26},{10... | collective-permute-start | bytes 589832 | tf_op jit(solution)/shard_map/ppermute | solution.py:23
  51.2 1.6 %collective-permute-start.9 = (f32[64,768]{1,0:T(8,128)S(1)}, f32[64,768]{1,0:T(8,128)S(1)}, u32[]{:S(2)}, u32[]{:S(2)}) collective-permute-start(f32[64,768]{1,0:T(8,128)S(1)} %pad_maximum_fusion.line0), channel_id=1, source_target_pairs={{0,16},{8,24},{16,0},{24,8},{1,17},{9,25},{17,1},{25,9},{2,18},{10... | collective-permute-start | bytes 589832 | tf_op jit(solution)/shard_map/ppermute | solution.py:23
  52.9 2.8 %shard_map.38.places = s32[512]{0:T(512)S(1)} custom-call(s32[4096]{0:T(1024)S(1)} %get-tuple-element.16.order, s32[4]{0:T(128)S(1)} %pad_add_fusion.where_am_i), custom_call_target="tpu_custom_call" | custom-call | tf_op jit(solution)/shard_map/pallas_call | solution.py:377
  55.6 3.9 %collective-permute-done.10.line3 = f32[64,768]{1,0:T(8,128)S(1)} collective-permute-done((f32[64,768]{1,0:T(8,128)S(1)}, f32[64,768]{1,0:T(8,128)S(1)}, u32[]{:S(2)}, u32[]{:S(2)}) %collective-permute-start.10) | collective-permute-done | bytes 196640 | tf_op jit(solution)/shard_map/ppermute | solution.py:23
  59.5 3.3 %collective-permute-done.8.line1 = f32[64,768]{1,0:T(8,128)S(1)} collective-permute-done((f32[64,768]{1,0:T(8,128)S(1)}, f32[64,768]{1,0:T(8,128)S(1)}, u32[]{:S(2)}, u32[]{:S(2)}) %collective-permute-start.8) | collective-permute-done | bytes 196640 | tf_op jit(solution)/shard_map/ppermute | solution.py:23
  62.8 3.9 %shard_map.41.w_ref = bf16[512,768]{1,0:T(8,128)(2,1)S(1)} custom-call(s32[4]{0:T(128)S(1)} %pad_add_fusion.where_am_i, f32[64,768]{1,0:T(8,128)S(1)} %pad_maximum_fusion.line0, f32[64,768]{1,0:T(8,128)S(1)} %collective-permute-done.8.line1, f32[64,768]{1,0:T(8,128)S(1)} %collective-permute-done.9.line2, f32[64,768]{1,0:T(8,128)S(1)} %collective-permute-done.10.line3), custom_call_target="tpu_custom_call" | custom-call | tf_op jit(solution)/shard_map/pallas_call | solution.py:319
  66.7 2.5 %shard_map.44 = f32[512,512]{1,0:T(8,128)} custom-call(s32[4]{0:T(128)S(1)} %pad_add_fusion.where_am_i, s32[512]{0:T(512)S(1)} %shard_map.38.places, f32[512,512]{1,0:T(8,128)S(1)} %copy-done, bf16[512,768]{1,0:T(8,128)(2,1)S(1)} %shard_map.41.w_ref, f32[128,512]{1,0:T(8,128)S(1)} %get-tuple-element.24.pivot_half, ...), custom_call_target="tpu_custom_call" | custom-call | tf_op jit(solution)/shard_map/pallas_call | solution.py:379
  (31 shorter events, 2.5 us)
Async XLA Ops:
  0.0 7.7 %collective-permute-start = (f32[8,512]{1,0:T(8,128)}, f32[8,512]{1,0:T(8,128)S(1)}, u32[]{:S(2)}, u32[]{:S(2)}) collective-permute-start(f32[8,512]{1,0:T(8,128)} %bitcast.5), channel_id=1, source_target_pairs={{0,1},{1,2},{2,3},{3,4},{4,5},{5,6},{6,7},{7,0},{8,9},{9,10},{10,1... | collective-permute-start | bytes 49160 | tf_op jit(solution)/shard_map/ppermute | solution.py:23
  2.5 5.3 %collective-permute-start.1 = (f32[8,512]{1,0:T(8,128)}, f32[8,512]{1,0:T(8,128)S(1)}, u32[]{:S(2)}, u32[]{:S(2)}) collective-permute-start(f32[8,512]{1,0:T(8,128)} %bitcast.6), channel_id=1, source_target_pairs={{0,7},{1,0},{2,1},{3,2},{4,3},{5,4},{6,5},{7,6},{8,15},{9,8},{10,9... | collective-permute-start | bytes 49160 | tf_op jit(solution)/shard_map/ppermute | solution.py:23
  7.7 0.7 %copy-start.1 = (f32[512,8]{0,1:T(8,128)S(1)}, f32[512,8]{0,1:T(8,128)}, u32[]{:S(2)}) copy-start(f32[512,8]{0,1:T(8,128)} %param.4) | copy-start | bytes 49156
  8.5 8.9 %collective-permute-start.2 = (f32[24,512]{1,0:T(8,128)S(1)}, f32[24,512]{1,0:T(8,128)S(1)}, u32[]{:S(2)}, u32[]{:S(2)}) collective-permute-start(f32[24,512]{1,0:T(8,128)S(1)} %get-tuple-element.17.three), channel_id=1, source_target_pairs={{0,3},{1,4},{2,5},{3,6},{4,7},{5,0},{6,1},{7,2},{8,11},{9,12},{10,... | collective-permute-start | bytes 147464 | tf_op jit(solution)/shard_map/ppermute | solution.py:23
  12.7 4.6 %collective-permute-start.3 = (f32[16,512]{1,0:T(8,128)S(1)}, f32[16,512]{1,0:T(8,128)S(1)}, u32[]{:S(2)}, u32[]{:S(2)}) collective-permute-start(f32[16,512]{1,0:T(8,128)S(1)} %get-tuple-element.18), channel_id=1, source_target_pairs={{0,5},{1,6},{2,7},{3,0},{4,1},{5,2},{6,3},{7,4},{8,13},{9,14},{10,... | collective-permute-start | bytes 98312 | tf_op jit(solution)/shard_map/ppermute | solution.py:23
  17.3 9.3 %collective-permute-start.4 = (f32[64,256]{1,0:T(8,128)S(1)}, f32[64,256]{1,0:T(8,128)S(1)}, u32[]{:S(2)}, u32[]{:S(2)}) collective-permute-start(f32[64,256]{1,0:T(8,128)S(1)} %get-tuple-element.20), channel_id=1, source_target_pairs={{0,32},{32,0},{1,33},{33,1},{2,34},{34,2},{3,35},{35,3},{4,36},{36... | collective-permute-start | bytes 196616 | tf_op jit(solution)/shard_map/ppermute | solution.py:27
  21.0 0.7 copy-start.2
  26.5 3.8 %collective-permute-start.11 = (f32[128,512]{1,0:T(8,128)S(1)}, f32[128,512]{1,0:T(8,128)S(1)}, u32[]{:S(2)}, u32[]{:S(2)}) collective-permute-start(f32[128,512]{1,0:T(8,128)S(1)} %get-tuple-element.22.send), channel_id=1, source_target_pairs={{0,32},{32,0},{1,33},{33,1},{2,34},{34,2},{3,35},{35,3},{4,36},{36... | collective-permute-start | bytes 786440 | tf_op jit(solution)/shard_map/ppermute | solution.py:27
  26.6 7.1 %collective-permute-start.5 = (f32[64,256]{1,0:T(8,128)S(1)}, f32[64,256]{1,0:T(8,128)S(1)}, u32[]{:S(2)}, u32[]{:S(2)}) collective-permute-start(f32[64,256]{1,0:T(8,128)S(1)} %broadcast_select_fusion), channel_id=1, source_target_pairs={{0,128},{64,192},{128,0},{192,64},{1,129},{65,193},{129,1},{193,65... | collective-permute-start | bytes 196616 | tf_op jit(solution)/shard_map/ppermute | solution.py:23
  29.4 4.2 %collective-permute-start.6 = (f32[64,256]{1,0:T(8,128)S(1)}, f32[64,256]{1,0:T(8,128)S(1)}, u32[]{:S(2)}, u32[]{:S(2)}) collective-permute-start(f32[64,256]{1,0:T(8,128)S(1)} %broadcast_select_fusion), channel_id=1, source_target_pairs={{0,64},{32,224},{64,128},{96,32},{128,192},{160,96},{192,0},{224,1... | collective-permute-start | bytes 196616 | tf_op jit(solution)/shard_map/ppermute | solution.py:312
  30.9 9.4 %collective-permute-start.12 = (f32[128,512]{1,0:T(8,128)S(1)}, f32[128,512]{1,0:T(8,128)S(1)}, u32[]{:S(2)}, u32[]{:S(2)}) collective-permute-start(f32[128,512]{1,0:T(8,128)S(1)} %shard_map.42.joined), channel_id=1, source_target_pairs={{0,64},{64,128},{128,192},{192,0},{1,65},{65,129},{129,193},{193,1... | collective-permute-start | bytes 786440 | tf_op jit(solution)/shard_map/ppermute | solution.py:23
  31.6 8.8 %collective-permute-start.13 = (f32[128,512]{1,0:T(8,128)S(1)}, f32[128,512]{1,0:T(8,128)S(1)}, u32[]{:S(2)}, u32[]{:S(2)}) collective-permute-start(f32[128,512]{1,0:T(8,128)S(1)} %shard_map.42.joined), channel_id=1, source_target_pairs={{0,192},{64,0},{128,64},{192,128},{1,193},{65,1},{129,65},{193,129... | collective-permute-start | bytes 786440 | tf_op jit(solution)/shard_map/ppermute | solution.py:23
  33.7 9.5 %collective-permute-start.7 = (f32[64,256]{1,0:T(8,128)S(1)}, f32[64,256]{1,0:T(8,128)S(1)}, u32[]{:S(2)}, u32[]{:S(2)}) collective-permute-start(f32[64,256]{1,0:T(8,128)S(1)} %select_select_fusion), channel_id=1, source_target_pairs={{0,32},{32,0},{1,33},{33,1},{2,34},{34,2},{3,35},{35,3},{4,36},{36... | collective-permute-start | bytes 196616 | tf_op jit(solution)/shard_map/ppermute | solution.py:27
  40.3 5.1 %collective-permute-start.14 = (f32[64,512]{1,0:T(8,128)S(1)}, f32[64,512]{1,0:T(8,128)S(1)}, u32[]{:S(2)}, u32[]{:S(2)}) collective-permute-start(f32[64,512]{1,0:T(8,128)S(1)} %slice.8), channel_id=1, source_target_pairs={{0,64},{64,128},{128,192},{192,0},{1,65},{65,129},{129,193},{193,1... | collective-permute-start | bytes 393224 | tf_op jit(solution)/shard_map/ppermute | solution.py:23
  40.5 5.0 %collective-permute-start.15 = (f32[64,512]{1,0:T(8,128)S(1)}, f32[64,512]{1,0:T(8,128)S(1)}, u32[]{:S(2)}, u32[]{:S(2)}) collective-permute-start(f32[64,512]{1,0:T(8,128)S(1)} %slice.9), channel_id=1, source_target_pairs={{0,192},{64,0},{128,64},{192,128},{1,193},{65,1},{129,65},{193,129... | collective-permute-start | bytes 393224 | tf_op jit(solution)/shard_map/ppermute | solution.py:23
  46.2 20.5 %copy-start = (f32[512,512]{1,0:T(8,128)S(1)}, f32[512,512]{1,0:T(8,128)}, u32[]{:S(2)}) copy-start(f32[512,512]{1,0:T(8,128)} %t_ref.1) | copy-start | bytes 3145732
  46.2 20.5 %collective-permute-start.16 = (f32[128,512]{1,0:T(8,128)S(1)}, f32[128,512]{1,0:T(8,128)S(1)}, u32[]{:S(2)}, u32[]{:S(2)}) collective-permute-start(f32[128,512]{1,0:T(8,128)S(1)} %get-tuple-element.26), channel_id=1, source_target_pairs={{0,32},{32,0},{1,33},{33,1},{2,34},{34,2},{3,35},{35,3},{4,36},{36... | collective-permute-start | bytes 786440 | tf_op jit(solution)/shard_map/ppermute | solution.py:27
  48.4 11.1 %collective-permute-start.10 = (f32[64,768]{1,0:T(8,128)S(1)}, f32[64,768]{1,0:T(8,128)S(1)}, u32[]{:S(2)}, u32[]{:S(2)}) collective-permute-start(f32[64,768]{1,0:T(8,128)S(1)} %pad_maximum_fusion.line0), channel_id=1, source_target_pairs={{0,24},{8,0},{16,8},{24,16},{1,25},{9,1},{17,9},{25,17},{2,26},{10... | collective-permute-start | bytes 589832 | tf_op jit(solution)/shard_map/ppermute | solution.py:23
  51.2 11.6 %collective-permute-start.8 = (f32[64,768]{1,0:T(8,128)S(1)}, f32[64,768]{1,0:T(8,128)S(1)}, u32[]{:S(2)}, u32[]{:S(2)}) collective-permute-start(f32[64,768]{1,0:T(8,128)S(1)} %pad_maximum_fusion.line0), channel_id=1, source_target_pairs={{0,8},{8,16},{16,24},{24,0},{1,9},{9,17},{17,25},{25,1},{2,10},{10... | collective-permute-start | bytes 589832 | tf_op jit(solution)/shard_map/ppermute | solution.py:23
  51.2 11.6 %collective-permute-start.9 = (f32[64,768]{1,0:T(8,128)S(1)}, f32[64,768]{1,0:T(8,128)S(1)}, u32[]{:S(2)}, u32[]{:S(2)}) collective-permute-start(f32[64,768]{1,0:T(8,128)S(1)} %pad_maximum_fusion.line0), channel_id=1, source_target_pairs={{0,16},{8,24},{16,0},{24,8},{1,17},{9,25},{17,1},{25,9},{2,18},{10... | collective-permute-start | bytes 589832 | tf_op jit(solution)/shard_map/ppermute | solution.py:23

commit v5 on v4

--- a/solution.py
+++ b/solution.py
@@ -311,11 +311,12 @@
     ways = [(i, (i + (2 if i % 2 == 0 else 6)) % 8) for i in range(8)]
     near = lax.ppermute(square, ROW, ways)
     far = along(square, "x", 2)
+    moved = swapped(near, "core", 1)
+    near = jnp.where(core == chip >> 1, near, moved)
     square = jnp.where(chip == 0, square, jnp.where(chip == 2, far, near))
-    moved = swapped(square, "core", 1)
-    square = jnp.where((chip & 1 == 1) & (core == (chip >> 1 ^ 1)), moved, square)
     line = jnp.concatenate([panels, square], axis=1)
-    lines = [along(line, "y", step) for step in (1, 2, 3)]
+    second = along(line, "y", 2)
+    lines = [along(line, "y", 1), second, along(line, "y", 3)]
     weights = pl.pallas_call(
         weights_kernel,
         out_shape=jax.ShapeDtypeStruct((rows, 3 * width), jnp.bfloat16),
@@ -342,8 +343,9 @@
         ],
         compiler_params=PARAMS,
     )
+    targets = jnp.minimum(pivots, rows * 8 - 1)
     keep, send, meta, order = plan(
-        pivots, here, pltpu.with_memory_space_constraint(trailing, pltpu.HBM)
+        targets, here, pltpu.with_memory_space_constraint(trailing, pltpu.HBM)
     )
     got = swapped(send, "core", 1)
     combine = pl.pallas_call(
@@ -355,8 +357,8 @@
     )
     joined = combine(here, keep, got, meta)
     near_before, near_after = along(joined, "x", 1), along(joined, "x", -1)
+    far_high = along(near_after[half // 2 :], "x", -1)
     far_low = along(near_before[: half // 2], "x", 1)
-    far_high = along(near_after[half // 2 :], "x", -1)
     halves = pl.pallas_call(
         halves_kernel,
         out_shape=(f32(half, columns),) * 3,

time: 69.8 us -> 67.2 us (0.963)
  starting transfers between devices: 33 us -> 29.3 us
  waiting for transfers between devices: 19.3 us -> 21.5 us
    ppermute x1, waiting for transfers between devices: 0.01 us -> 5.62 us  [device_step(): near = lax.ppermute(square, ROW, ways)]
    ppermute x12, starting transfers between devices: 23.7 us -> 19.8 us  [along(): lax.ppermute(value, axis, [(i, (i + step) % size) for i in range(size)])]
    ppermute x12, waiting for transfers between devices: 19.3 us -> 15.8 us  [along(): lax.ppermute(value, axis, [(i, (i + step) % size) for i in range(size)])]
  transfers between devices with their start and end apart: 17 -> 17, of which waited for: 6 -> 6; matrix products, arithmetic and copies ran while one was open for 0% -> 0% of each run, Pallas kernels for 17% -> 11%
where the time goes in v5:
time: 67.2 us; the launch traced here: 67.1 us
  starting transfers between devices  29.3 us (44%)
  waiting for transfers between devices  21.5 us (32%)
  Pallas kernels  15.3 us (23%)
  local copies, waits for them, and re-layouts  0.71 us (1%)
    ppermute x12, starting transfers between devices, along(): lax.ppermute(value, axis, [(i, (i + step) % size) for i in range(size)])  19.8 us
    ppermute x12, waiting for transfers between devices, along(): lax.ppermute(value, axis, [(i, (i + step) % size) for i in range(size)])  15.8 us
    ppermute x4, starting transfers between devices, swapped(): lax.ppermute(value, axis, [(i, i ^ bit) for i in range(lax.axis_size(axis...  8.15 us
    ppermute x1, waiting for transfers between devices, device_step(): near = lax.ppermute(square, ROW, ways)  5.62 us
    pallas_call x1, Pallas kernels, device_step(): plan(targets, here, pltpu.with_memory_space_constraint(trailing, pltpu.HBM))  4.84 us
    pallas_call x1, Pallas kernels, device_step(): pl.pallas_call(weights_kernel, out_shape=jax.ShapeDtypeStruct((rows, 3 *...  3.88 us
    pallas_call x1, Pallas kernels, device_step(): places = listing(order, here)  2.75 us
    pallas_call x1, Pallas kernels, device_step(): pl.pallas_call(final_kernel, out_shape=f32(rows, columns), in_specs=[SMEM...  2.51 us
  transfers between devices with their start and end apart: 17, of which 6 were waited for; matrix products, arithmetic and copies ran while one was open for 0% of the time, Pallas kernels for 11%

profile of v5, /device:TPU:1, one launch (start us, length us, event | category | flops | bytes accessed | tf_op | source)
XLA Modules:
  0.0 67.1 jit_solution(13209678235744738935)
XLA Ops:
  0.0 0.7 %copy-done.2 = s32[256]{0:T(256)S(1)} copy-done((s32[256]{0:T(256)S(1)}, s32[256]{0:T(256)}, u32[]{:S(2)}) %copy-start.2) | copy-done | bytes 1048
  0.8 4.8 %shard_map.37 = (f32[128,512]{1,0:T(8,128)S(1)}, f32[128,512]{1,0:T(8,128)S(1)}, s32[256,128]{1,0:T(8,128)S(1)}, s32[4096]{0:T(1024)S(1)}) custom-call(s32[256]{0:T(256)S(1)} %broadcast_minimum_fusion.piv, s32[4]{0:T(128)S(1)} %pad_add_fusion.where_am_i, f32[512,512]{1,0:T(8,128)} %t_ref.1), custom_call_target="tpu_custom_call" | custom-call | tf_op jit(solution)/shard_map/pallas_call | solution.py:347
  5.6 3.3 %collective-permute-start.11 = (f32[128,512]{1,0:T(8,128)S(1)}, f32[128,512]{1,0:T(8,128)S(1)}, u32[]{:S(2)}, u32[]{:S(2)}) collective-permute-start(f32[128,512]{1,0:T(8,128)S(1)} %get-tuple-element.22.send), channel_id=1, source_target_pairs={{0,32},{32,0},{1,33},{33,1},{2,34},{34,2},{3,35},{35,3},{4,36},{36... | collective-permute-start | bytes 786440 | tf_op jit(solution)/shard_map/ppermute | solution.py:27
  8.9 3.9 %collective-permute-start.1 = (f32[8,512]{1,0:T(8,128)S(1)}, f32[8,512]{1,0:T(8,128)S(1)}, u32[]{:S(2)}, u32[]{:S(2)}) collective-permute-start(f32[8,512]{1,0:T(8,128)S(1)} %bitcast.6), channel_id=1, source_target_pairs={{0,7},{1,0},{2,1},{3,2},{4,3},{5,4},{6,5},{7,6},{8,15},{9,8},{10,9... | collective-permute-start | bytes 49160 | tf_op jit(solution)/shard_map/ppermute | solution.py:23
  12.8 1.1 %collective-permute-done.before = f32[8,512]{1,0:T(8,128)S(1)} collective-permute-done((f32[8,512]{1,0:T(8,128)S(1)}, f32[8,512]{1,0:T(8,128)S(1)}, u32[]{:S(2)}, u32[]{:S(2)}) %collective-permute-start) | collective-permute-done | bytes 16416 | tf_op jit(solution)/shard_map/ppermute | solution.py:23
  13.9 4.3 %collective-permute-start.2 = (f32[24,512]{1,0:T(8,128)S(1)}, f32[24,512]{1,0:T(8,128)S(1)}, u32[]{:S(2)}, u32[]{:S(2)}) collective-permute-start(f32[24,512]{1,0:T(8,128)S(1)} %get-tuple-element.17.three), channel_id=1, source_target_pairs={{0,3},{1,4},{2,5},{3,6},{4,7},{5,0},{6,1},{7,2},{8,11},{9,12},{10,... | collective-permute-start | bytes 147464 | tf_op jit(solution)/shard_map/ppermute | solution.py:23
  18.5 4.3 %collective-permute-done.3.far_after = f32[16,512]{1,0:T(8,128)S(1)} collective-permute-done((f32[16,512]{1,0:T(8,128)S(1)}, f32[16,512]{1,0:T(8,128)S(1)}, u32[]{:S(2)}, u32[]{:S(2)}) %collective-permute-start.3) | collective-permute-done | bytes 32800 | tf_op jit(solution)/shard_map/ppermute | solution.py:23
  22.8 3.0 %collective-permute-start.4 = (f32[64,256]{1,0:T(8,128)S(1)}, f32[64,256]{1,0:T(8,128)S(1)}, u32[]{:S(2)}, u32[]{:S(2)}) collective-permute-start(f32[64,256]{1,0:T(8,128)S(1)} %get-tuple-element.20), channel_id=1, source_target_pairs={{0,32},{32,0},{1,33},{33,1},{2,34},{34,2},{3,35},{35,3},{4,36},{36... | collective-permute-start | bytes 196616 | tf_op jit(solution)/shard_map/ppermute | solution.py:27
  26.4 1.3 %collective-permute-start.12 = (f32[128,512]{1,0:T(8,128)S(1)}, f32[128,512]{1,0:T(8,128)S(1)}, u32[]{:S(2)}, u32[]{:S(2)}) collective-permute-start(f32[128,512]{1,0:T(8,128)S(1)} %shard_map.42.joined), channel_id=1, source_target_pairs={{0,64},{64,128},{128,192},{192,0},{1,65},{65,129},{129,193},{193,1... | collective-permute-start | bytes 786440 | tf_op jit(solution)/shard_map/ppermute | solution.py:23
  27.7 1.5 %collective-permute-start.13 = (f32[128,512]{1,0:T(8,128)S(1)}, f32[128,512]{1,0:T(8,128)S(1)}, u32[]{:S(2)}, u32[]{:S(2)}) collective-permute-start(f32[128,512]{1,0:T(8,128)S(1)} %shard_map.42.joined), channel_id=1, source_target_pairs={{0,192},{64,0},{128,64},{192,128},{1,193},{65,1},{129,65},{193,129... | collective-permute-start | bytes 786440 | tf_op jit(solution)/shard_map/ppermute | solution.py:23
  29.2 1.3 %collective-permute-start.6 = (f32[64,256]{1,0:T(8,128)S(1)}, f32[64,256]{1,0:T(8,128)S(1)}, u32[]{:S(2)}, u32[]{:S(2)}) collective-permute-start(f32[64,256]{1,0:T(8,128)S(1)} %broadcast_select_fusion), channel_id=1, source_target_pairs={{0,64},{32,224},{64,128},{96,32},{128,192},{160,96},{192,0},{224,1... | collective-permute-start | bytes 196616 | tf_op jit(solution)/shard_map/ppermute | solution.py:312
  31.1 5.6 %collective-permute-done.6 = f32[64,256]{1,0:T(8,128)S(1)} collective-permute-done((f32[64,256]{1,0:T(8,128)S(1)}, f32[64,256]{1,0:T(8,128)S(1)}, u32[]{:S(2)}, u32[]{:S(2)}) %collective-permute-start.6) | collective-permute-done | bytes 65568 | tf_op jit(solution)/shard_map/ppermute | solution.py:312
  37.4 0.6 collective-permute-start.14
  38.0 3.0 %collective-permute-start.15 = (f32[64,512]{1,0:T(8,128)S(1)}, f32[64,512]{1,0:T(8,128)S(1)}, u32[]{:S(2)}, u32[]{:S(2)}) collective-permute-start(f32[64,512]{1,0:T(8,128)S(1)} %slice.9), channel_id=1, source_target_pairs={{0,192},{64,0},{128,64},{192,128},{1,193},{65,1},{129,65},{193,129... | collective-permute-start | bytes 393224 | tf_op jit(solution)/shard_map/ppermute | solution.py:23
  41.0 3.2 %collective-permute-done.14.low = f32[64,512]{1,0:T(8,128)S(1)} collective-permute-done((f32[64,512]{1,0:T(8,128)S(1)}, f32[64,512]{1,0:T(8,128)S(1)}, u32[]{:S(2)}, u32[]{:S(2)}) %collective-permute-start.14) | collective-permute-done | bytes 131104 | tf_op jit(solution)/shard_map/ppermute | solution.py:23
  44.2 0.7 %shard_map.43 = (f32[128,512]{1,0:T(8,128)S(1)}, f32[128,512]{1,0:T(8,128)S(1)}, f32[128,512]{1,0:T(8,128)S(1)}) custom-call(s32[4]{0:T(128)S(1)} %pad_add_fusion.where_am_i, f32[128,512]{1,0:T(8,128)S(1)} %shard_map.42.joined, f32[128,512]{1,0:T(8,128)S(1)} %collective-permute-done.12.before, f32[128,512]{1,0:T(8,128)S(1)} %collective-permute-done.13.after, ...), custom_call_target="tpu_custom_call" | custom-call | tf_op jit(solution)/shard_map/pallas_call | solution.py:369
  45.0 1.2 %collective-permute-start.16 = (f32[128,512]{1,0:T(8,128)S(1)}, f32[128,512]{1,0:T(8,128)S(1)}, u32[]{:S(2)}, u32[]{:S(2)}) collective-permute-start(f32[128,512]{1,0:T(8,128)S(1)} %get-tuple-element.26), channel_id=1, source_target_pairs={{0,32},{32,0},{1,33},{33,1},{2,34},{34,2},{3,35},{35,3},{4,36},{36... | collective-permute-start | bytes 786440 | tf_op jit(solution)/shard_map/ppermute | solution.py:27
  46.2 2.8 %collective-permute-start.10 = (f32[64,768]{1,0:T(8,128)S(1)}, f32[64,768]{1,0:T(8,128)S(1)}, u32[]{:S(2)}, u32[]{:S(2)}) collective-permute-start(f32[64,768]{1,0:T(8,128)S(1)} %pad_maximum_fusion.line0), channel_id=1, source_target_pairs={{0,24},{8,0},{16,8},{24,16},{1,25},{9,1},{17,9},{25,17},{2,26},{10... | collective-permute-start | bytes 589832 | tf_op jit(solution)/shard_map/ppermute | solution.py:23
  49.0 1.6 %collective-permute-start.9 = (f32[64,768]{1,0:T(8,128)S(1)}, f32[64,768]{1,0:T(8,128)S(1)}, u32[]{:S(2)}, u32[]{:S(2)}) collective-permute-start(f32[64,768]{1,0:T(8,128)S(1)} %pad_maximum_fusion.line0), channel_id=1, source_target_pairs={{0,16},{8,24},{16,0},{24,8},{1,17},{9,25},{17,1},{25,9},{2,18},{10... | collective-permute-start | bytes 589832 | tf_op jit(solution)/shard_map/ppermute | solution.py:23
  50.6 2.8 %shard_map.38.places = s32[512]{0:T(512)S(1)} custom-call(s32[4096]{0:T(1024)S(1)} %get-tuple-element.16.order, s32[4]{0:T(128)S(1)} %pad_add_fusion.where_am_i), custom_call_target="tpu_custom_call" | custom-call | tf_op jit(solution)/shard_map/pallas_call | solution.py:379
  53.4 3.9 %collective-permute-done.10.line3 = f32[64,768]{1,0:T(8,128)S(1)} collective-permute-done((f32[64,768]{1,0:T(8,128)S(1)}, f32[64,768]{1,0:T(8,128)S(1)}, u32[]{:S(2)}, u32[]{:S(2)}) %collective-permute-start.10) | collective-permute-done | bytes 196640 | tf_op jit(solution)/shard_map/ppermute | solution.py:23
  57.3 3.3 %collective-permute-done.8.line1 = f32[64,768]{1,0:T(8,128)S(1)} collective-permute-done((f32[64,768]{1,0:T(8,128)S(1)}, f32[64,768]{1,0:T(8,128)S(1)}, u32[]{:S(2)}, u32[]{:S(2)}) %collective-permute-start.8) | collective-permute-done | bytes 196640 | tf_op jit(solution)/shard_map/ppermute | solution.py:23
  60.5 3.9 %shard_map.41.w_ref = bf16[512,768]{1,0:T(8,128)(2,1)S(1)} custom-call(s32[4]{0:T(128)S(1)} %pad_add_fusion.where_am_i, f32[64,768]{1,0:T(8,128)S(1)} %pad_maximum_fusion.line0, f32[64,768]{1,0:T(8,128)S(1)} %collective-permute-done.8.line1, f32[64,768]{1,0:T(8,128)S(1)} %collective-permute-done.9.line2, f32[64,768]{1,0:T(8,128)S(1)} %collective-permute-done.10.line3), custom_call_target="tpu_custom_call" | custom-call | tf_op jit(solution)/shard_map/pallas_call | solution.py:320
  64.5 2.5 %shard_map.44 = f32[512,512]{1,0:T(8,128)} custom-call(s32[4]{0:T(128)S(1)} %pad_add_fusion.where_am_i, s32[512]{0:T(512)S(1)} %shard_map.38.places, f32[512,512]{1,0:T(8,128)S(1)} %copy-done, bf16[512,768]{1,0:T(8,128)(2,1)S(1)} %shard_map.41.w_ref, f32[128,512]{1,0:T(8,128)S(1)} %get-tuple-element.24.pivot_half, ...), custom_call_target="tpu_custom_call" | custom-call | tf_op jit(solution)/shard_map/pallas_call | solution.py:381
  (31 shorter events, 2.2 us)
Async XLA Ops:
  0.0 0.7 %copy-start.2 = (s32[256]{0:T(256)S(1)}, s32[256]{0:T(256)}, u32[]{:S(2)}) copy-start(s32[256]{0:T(256)} %param.5) | copy-start | bytes 3076
  0.8 8.1 %copy-start.1 = (f32[512,8]{0,1:T(8,128)S(1)}, f32[512,8]{0,1:T(8,128)}, u32[]{:S(2)}) copy-start(f32[512,8]{0,1:T(8,128)} %param.4) | copy-start | bytes 49156
  5.6 20.2 %collective-permute-start.11 = (f32[128,512]{1,0:T(8,128)S(1)}, f32[128,512]{1,0:T(8,128)S(1)}, u32[]{:S(2)}, u32[]{:S(2)}) collective-permute-start(f32[128,512]{1,0:T(8,128)S(1)} %get-tuple-element.22.send), channel_id=1, source_target_pairs={{0,32},{32,0},{1,33},{33,1},{2,34},{34,2},{3,35},{35,3},{4,36},{36... | collective-permute-start | bytes 786440 | tf_op jit(solution)/shard_map/ppermute | solution.py:27
  8.9 5.0 %collective-permute-start = (f32[8,512]{1,0:T(8,128)S(1)}, f32[8,512]{1,0:T(8,128)S(1)}, u32[]{:S(2)}, u32[]{:S(2)}) collective-permute-start(f32[8,512]{1,0:T(8,128)S(1)} %bitcast.5), channel_id=1, source_target_pairs={{0,1},{1,2},{2,3},{3,4},{4,5},{5,6},{6,7},{7,0},{8,9},{9,10},{10,1... | collective-permute-start | bytes 49160 | tf_op jit(solution)/shard_map/ppermute | solution.py:23
  8.9 5.0 %collective-permute-start.1 = (f32[8,512]{1,0:T(8,128)S(1)}, f32[8,512]{1,0:T(8,128)S(1)}, u32[]{:S(2)}, u32[]{:S(2)}) collective-permute-start(f32[8,512]{1,0:T(8,128)S(1)} %bitcast.6), channel_id=1, source_target_pairs={{0,7},{1,0},{2,1},{3,2},{4,3},{5,4},{6,5},{7,6},{8,15},{9,8},{10,9... | collective-permute-start | bytes 49160 | tf_op jit(solution)/shard_map/ppermute | solution.py:23
  13.9 8.9 %collective-permute-start.2 = (f32[24,512]{1,0:T(8,128)S(1)}, f32[24,512]{1,0:T(8,128)S(1)}, u32[]{:S(2)}, u32[]{:S(2)}) collective-permute-start(f32[24,512]{1,0:T(8,128)S(1)} %get-tuple-element.17.three), channel_id=1, source_target_pairs={{0,3},{1,4},{2,5},{3,6},{4,7},{5,0},{6,1},{7,2},{8,11},{9,12},{10,... | collective-permute-start | bytes 147464 | tf_op jit(solution)/shard_map/ppermute | solution.py:23
  18.2 4.6 %collective-permute-start.3 = (f32[16,512]{1,0:T(8,128)S(1)}, f32[16,512]{1,0:T(8,128)S(1)}, u32[]{:S(2)}, u32[]{:S(2)}) collective-permute-start(f32[16,512]{1,0:T(8,128)S(1)} %get-tuple-element.18), channel_id=1, source_target_pairs={{0,5},{1,6},{2,7},{3,0},{4,1},{5,2},{6,3},{7,4},{8,13},{9,14},{10,... | collective-permute-start | bytes 98312 | tf_op jit(solution)/shard_map/ppermute | solution.py:23
  22.8 6.4 %collective-permute-start.4 = (f32[64,256]{1,0:T(8,128)S(1)}, f32[64,256]{1,0:T(8,128)S(1)}, u32[]{:S(2)}, u32[]{:S(2)}) collective-permute-start(f32[64,256]{1,0:T(8,128)S(1)} %get-tuple-element.20), channel_id=1, source_target_pairs={{0,32},{32,0},{1,33},{33,1},{2,34},{34,2},{3,35},{35,3},{4,36},{36... | collective-permute-start | bytes 196616 | tf_op jit(solution)/shard_map/ppermute | solution.py:27
  26.4 10.9 %collective-permute-start.12 = (f32[128,512]{1,0:T(8,128)S(1)}, f32[128,512]{1,0:T(8,128)S(1)}, u32[]{:S(2)}, u32[]{:S(2)}) collective-permute-start(f32[128,512]{1,0:T(8,128)S(1)} %shard_map.42.joined), channel_id=1, source_target_pairs={{0,64},{64,128},{128,192},{192,0},{1,65},{65,129},{129,193},{193,1... | collective-permute-start | bytes 786440 | tf_op jit(solution)/shard_map/ppermute | solution.py:23
  27.7 10.3 %collective-permute-start.13 = (f32[128,512]{1,0:T(8,128)S(1)}, f32[128,512]{1,0:T(8,128)S(1)}, u32[]{:S(2)}, u32[]{:S(2)}) collective-permute-start(f32[128,512]{1,0:T(8,128)S(1)} %shard_map.42.joined), channel_id=1, source_target_pairs={{0,192},{64,0},{128,64},{192,128},{1,193},{65,1},{129,65},{193,129... | collective-permute-start | bytes 786440 | tf_op jit(solution)/shard_map/ppermute | solution.py:23
  29.2 7.5 %collective-permute-start.6 = (f32[64,256]{1,0:T(8,128)S(1)}, f32[64,256]{1,0:T(8,128)S(1)}, u32[]{:S(2)}, u32[]{:S(2)}) collective-permute-start(f32[64,256]{1,0:T(8,128)S(1)} %broadcast_select_fusion), channel_id=1, source_target_pairs={{0,64},{32,224},{64,128},{96,32},{128,192},{160,96},{192,0},{224,1... | collective-permute-start | bytes 196616 | tf_op jit(solution)/shard_map/ppermute | solution.py:312
  30.6 10.4 %collective-permute-start.5 = (f32[64,256]{1,0:T(8,128)S(1)}, f32[64,256]{1,0:T(8,128)S(1)}, u32[]{:S(2)}, u32[]{:S(2)}) collective-permute-start(f32[64,256]{1,0:T(8,128)S(1)} %broadcast_select_fusion), channel_id=1, source_target_pairs={{0,128},{64,192},{128,0},{192,64},{1,129},{65,193},{129,1},{193,65... | collective-permute-start | bytes 196616 | tf_op jit(solution)/shard_map/ppermute | solution.py:23
  36.7 4.3 %collective-permute-start.7 = (f32[64,256]{1,0:T(8,128)S(1)}, f32[64,256]{1,0:T(8,128)S(1)}, u32[]{:S(2)}, u32[]{:S(2)}) collective-permute-start(f32[64,256]{1,0:T(8,128)S(1)} %collective-permute-done.6), channel_id=1, source_target_pairs={{0,32},{32,0},{1,33},{33,1},{2,34},{34,2},{3,35},{35,3},{4,36},{36... | collective-permute-start | bytes 196616 | tf_op jit(solution)/shard_map/ppermute | solution.py:27
  37.4 6.9 %collective-permute-start.14 = (f32[64,512]{1,0:T(8,128)S(1)}, f32[64,512]{1,0:T(8,128)S(1)}, u32[]{:S(2)}, u32[]{:S(2)}) collective-permute-start(f32[64,512]{1,0:T(8,128)S(1)} %slice.8), channel_id=1, source_target_pairs={{0,64},{64,128},{128,192},{192,0},{1,65},{65,129},{129,193},{193,1... | collective-permute-start | bytes 393224 | tf_op jit(solution)/shard_map/ppermute | solution.py:23
  38.0 6.2 %collective-permute-start.15 = (f32[64,512]{1,0:T(8,128)S(1)}, f32[64,512]{1,0:T(8,128)S(1)}, u32[]{:S(2)}, u32[]{:S(2)}) collective-permute-start(f32[64,512]{1,0:T(8,128)S(1)} %slice.9), channel_id=1, source_target_pairs={{0,192},{64,0},{128,64},{192,128},{1,193},{65,1},{129,65},{193,129... | collective-permute-start | bytes 393224 | tf_op jit(solution)/shard_map/ppermute | solution.py:23
  44.9 19.5 %copy-start = (f32[512,512]{1,0:T(8,128)S(1)}, f32[512,512]{1,0:T(8,128)}, u32[]{:S(2)}) copy-start(f32[512,512]{1,0:T(8,128)} %t_ref.1) | copy-start | bytes 3145732
  45.0 19.5 %collective-permute-start.16 = (f32[128,512]{1,0:T(8,128)S(1)}, f32[128,512]{1,0:T(8,128)S(1)}, u32[]{:S(2)}, u32[]{:S(2)}) collective-permute-start(f32[128,512]{1,0:T(8,128)S(1)} %get-tuple-element.26), channel_id=1, source_target_pairs={{0,32},{32,0},{1,33},{33,1},{2,34},{34,2},{3,35},{35,3},{4,36},{36... | collective-permute-start | bytes 786440 | tf_op jit(solution)/shard_map/ppermute | solution.py:27
  46.2 11.1 %collective-permute-start.10 = (f32[64,768]{1,0:T(8,128)S(1)}, f32[64,768]{1,0:T(8,128)S(1)}, u32[]{:S(2)}, u32[]{:S(2)}) collective-permute-start(f32[64,768]{1,0:T(8,128)S(1)} %pad_maximum_fusion.line0), channel_id=1, source_target_pairs={{0,24},{8,0},{16,8},{24,16},{1,25},{9,1},{17,9},{25,17},{2,26},{10... | collective-permute-start | bytes 589832 | tf_op jit(solution)/shard_map/ppermute | solution.py:23
  49.0 11.6 %collective-permute-start.8 = (f32[64,768]{1,0:T(8,128)S(1)}, f32[64,768]{1,0:T(8,128)S(1)}, u32[]{:S(2)}, u32[]{:S(2)}) collective-permute-start(f32[64,768]{1,0:T(8,128)S(1)} %pad_maximum_fusion.line0), channel_id=1, source_target_pairs={{0,8},{8,16},{16,24},{24,0},{1,9},{9,17},{17,25},{25,1},{2,10},{10... | collective-permute-start | bytes 589832 | tf_op jit(solution)/shard_map/ppermute | solution.py:23
  49.0 11.6 %collective-permute-start.9 = (f32[64,768]{1,0:T(8,128)S(1)}, f32[64,768]{1,0:T(8,128)S(1)}, u32[]{:S(2)}, u32[]{:S(2)}) collective-permute-start(f32[64,768]{1,0:T(8,128)S(1)} %pad_maximum_fusion.line0), channel_id=1, source_target_pairs={{0,16},{8,24},{16,0},{24,8},{1,17},{9,25},{17,1},{25,9},{2,18},{10... | collective-permute-start | bytes 589832 | tf_op jit(solution)/shard_map/ppermute | solution.py:23
